TPU v7x, 128 devices: a whole 4x4x4 slice. The times are simulated.
128 devices in a mesh: freq: 4 (over z), row: 8 (over y, core), col: 4 (over x).
Axes of the slice: x: 4, y: 4, z: 4, core: 2. Of those that a mesh axis runs over, the one named last changes fastest.
Arguments:
- source_rows: bfloat16 [2, 16, 32, 4096], P(None, 'freq', 'row', 'col'), may hold values from -6 to 6
- data_matrix: bfloat16 [2, 16, 4096, 4096], P(None, 'freq', 'col', 'row'), may hold values from -0.0625 to 0.0625
- observed: bfloat16 [1024, 32, 4096], P(None, 'freq', ('row', 'col')), may hold values from -6 to 6
- window_owner: int32 [4, 32, 128, 1], P('freq', ('row', 'col')), may hold values from 0 to 127; in each aligned block of 128 rows (0 to 127, 128 to 255, ..., all dimensions but the last counted through in order) at most 2 rows name the same one
- filter_len: int32 [4, 32, 128], P('freq', ('row', 'col')), may hold values from 1 to 16, as said below
Outputs:
- primaries: bfloat16 [128, 128, 2, 64, 128], P(('freq', 'row', 'col'))
Inputs may be any that keep to these rules, and one draw needn't show every extreme that they name: `window_owner`: among the 128 windows of one (g, p), at most 2 share an owner, and exactly 2 do for some owner in some blocks. `filter_len`: some window has 16 taps and some has 1.
All inputs are finite; a program needn't handle non-finite values.
Results may differ from a plain program's by a relative error of at most 0.0051.
Values may be sent and summed in bfloat16 or wider, within the bound.
No kernel may reach another device: no remote copies, remote signals or barrier semaphores. Data moves between devices by JAX's collectives and lax.ppermute only.
A program may use at most 192 MiB of HBM per device.

v0:
```python
import math

import jax
import jax.numpy as jnp
from jax import lax
from jax.sharding import PartitionSpec as P

NT = 1024
WT = 64
WIN = 128
LMAX = 16
FIT_STEPS = 3


def joined_along(tiles, dim):
    tiles = jnp.moveaxis(tiles, 0, dim)
    shape = tiles.shape
    return tiles.reshape(*shape[:dim], shape[dim] * shape[dim + 1], *shape[dim + 2 :])


def sent_to_all(value, axis):
    peers = lax.axis_size(axis)
    return lax.all_to_all(
        jnp.broadcast_to(value[None], (peers, *value.shape)), axis, 0, 0, tiled=True
    )


def collect(value, axis, dim):
    return joined_along(sent_to_all(value, axis), dim)


def cut_along(value, dim, peers):
    shape = value.shape
    tiles = value.reshape(*shape[:dim], peers, shape[dim] // peers, *shape[dim + 1 :])
    return jnp.moveaxis(tiles, dim, 0)


def sum_at_owner(value, axis, dim):
    peers = lax.axis_size(axis)
    tiles = lax.all_to_all(cut_along(value, dim, peers), axis, 0, 0, tiled=True)
    return jnp.sum(tiles, axis=0)


def idft_table(bands, samples):
    freqs = (jnp.arange(bands) + 1).astype(jnp.float32)
    times = jnp.arange(samples).astype(jnp.float32)
    angle = 2.0 * math.pi * freqs[:, None] * times[None, :] / samples
    return jnp.stack([jnp.cos(angle), -jnp.sin(angle)]) * bands ** (-0.5)


def lagged(field, lag_index):
    if lag_index == 0:
        return field
    widths = [(0, 0)] * (field.ndim - 2) + [(lag_index, 0), (0, 0)]
    return jnp.pad(field[..., :-lag_index, :], widths)


def adapt(predicted_in, recorded_in, tap_in):
    samples = predicted_in.shape[-2]
    taps = tap_in.shape[-1]
    count = predicted_in.shape[0]
    later = jnp.arange(samples, dtype=jnp.int32)[:, None]
    sooner = jnp.arange(samples, dtype=jnp.int32)[None, :]
    lag_ids = jnp.arange(taps, dtype=jnp.int32)[:, None, None]
    diagonals = (
        ((later - sooner)[None] == lag_ids).astype(jnp.float32).reshape(taps, samples * samples)
    )

    def convolve(filter_taps):
        total = jnp.zeros(predicted_in.shape, jnp.float32)
        for lag_index in range(taps):
            total = total + filter_taps[:, lag_index, None, None] * lagged(predicted_in, lag_index)
        return total

    energy = jnp.sum(predicted_in * predicted_in, axis=(-2, -1))
    step_size = 0.4 / (energy + 1e-06)
    first = (jnp.arange(taps) == 0).astype(jnp.float32)
    filter_taps = tap_in * first
    residual = recorded_in - convolve(filter_taps)
    for sweep in range(FIT_STEPS):
        correl = jnp.einsum("wsj,wtj->wst", residual, predicted_in, precision=lax.Precision.HIGHEST)
        gradient = (
            jnp.dot(
                correl.reshape(count, samples * samples),
                diagonals.T,
                precision=lax.Precision.HIGHEST,
            )
            * tap_in
        )
        filter_taps = filter_taps + step_size[:, None] * gradient
        residual = recorded_in - convolve(filter_taps)
    return residual


def batched(left, right):
    return jnp.einsum("frk,fkc->frc", left, right, preferred_element_type=jnp.float32)


def window_form(field):
    samples, rows_here, receivers = field.shape
    shaped = field.reshape(samples // WT, WT, rows_here, receivers // WIN, WIN).transpose(
        2, 3, 0, 1, 4
    )
    return shaped.reshape(-1, WT, WIN)


def local(source_rows, data_matrix, observed, window_owner, filter_len):
    real_data = data_matrix[0]
    imag_data = data_matrix[1]
    panel_rows = collect(source_rows, "row", 2)
    real_part = batched(panel_rows[0], real_data) - batched(panel_rows[1], imag_data)
    imag_part = batched(panel_rows[0], imag_data) + batched(panel_rows[1], real_data)
    partial_terms = jnp.stack([real_part, imag_part])
    spectra = sum_at_owner(partial_terms, "col", 3).astype(jnp.bfloat16)
    spectrum = lax.all_to_all(spectra, "freq", split_axis=2, concat_axis=1, tiled=True)
    table = idft_table(spectrum.shape[1], NT)
    traces = jnp.einsum(
        "zfrc,zft->trc", spectrum.astype(jnp.float32), table, precision=lax.Precision.HIGHEST
    ).astype(jnp.bfloat16)
    predicted_win = window_form(traces)
    recorded_win = window_form(observed)
    owners = window_owner.reshape(-1)
    windows = owners.shape[0]
    devices = lax.axis_size("freq") * lax.axis_size("row") * lax.axis_size("col")
    slot_count = max(2, 2 * windows // devices)
    same_owner = owners[:, None] == owners[None, :]
    earlier = jnp.arange(windows)[None, :] < jnp.arange(windows)[:, None]
    slot_rank = jnp.sum(jnp.logical_and(same_owner, earlier), axis=1)
    target = owners * slot_count + slot_rank
    selector = (
        target[None, :] == jnp.arange(devices * slot_count, dtype=jnp.int32)[:, None]
    ).astype(jnp.bfloat16)
    tap_mask = (
        jnp.arange(LMAX, dtype=jnp.int32)[None, :] < filter_len.reshape(-1)[:, None]
    ).astype(jnp.float32)
    cleaned = adapt(
        predicted_win.astype(jnp.float32), recorded_win.astype(jnp.float32), tap_mask
    ).astype(jnp.bfloat16)
    buffer = jnp.einsum("sw,wtc->stc", selector, cleaned, preferred_element_type=jnp.float32)
    result = lax.all_to_all(
        buffer.astype(jnp.bfloat16).reshape(devices, slot_count, WT, WIN),
        ("freq", "row", "col"),
        split_axis=0,
        concat_axis=0,
        tiled=True,
    )
    return result[None]


def solution(mesh):
    return jax.shard_map(
        local,
        mesh=mesh,
        in_specs=(
            P(None, "freq", "row", "col"),
            P(None, "freq", "col", "row"),
            P(None, "freq", ("row", "col")),
            P("freq", ("row", "col"), None, None),
            P("freq", ("row", "col"), None),
        ),
        out_specs=P(("freq", "row", "col"), None, None, None, None),
        check_vma=False,
    )
```

profile of v0, /device:TPU:1, one launch (start us, length us, event | category | flops | bytes accessed | tf_op | source)
XLA Modules:
  0.0 282.8 jit_solution(8389520635523025036)
XLA Ops:
  0.0 1.9 broadcast_in_dim.4
  1.9 6.0 %all-to-all-start = ((bf16[8,2,4,4,1024]{4,3,2,1,0:T(4,128)(2,1)}), bf16[8,2,4,4,1024]{4,3,2,1,0:T(4,128)(2,1)S(1)}, u32[]{:S(2)}, u32[]{:S(2)}) async-start(bf16[8,2,4,4,1024]{4,3,2,1,0:T(4,128)(2,1)} %broadcast_in_dim.4), calls=%async_computation | async-start | bytes 1048576 | tf_op jit(solution)/shard_map/all_to_all | solution.py:23
  7.8 0.9 convert_reduce_fusion
  8.7 0.7 fusion.117
  9.5 0.3 fusion.114
  9.8 7.4 %all-to-all-done = bf16[8,2,4,4,1024]{4,3,2,1,0:T(4,128)(2,1)S(1)} async-done(((bf16[8,2,4,4,1024]{4,3,2,1,0:T(4,128)(2,1)}), bf16[8,2,4,4,1024]{4,3,2,1,0:T(4,128)(2,1)S(1)}, u32[]{:S(2)}, u32[]{:S(2)}) %all-to-all-start) | async-done | bytes 524320 | tf_op jit(solution)/shard_map/all_to_all | solution.py:23
  17.7 3.1 %fusion.39 = f32[4,32,512]{2,1,0:T(8,128)S(1)} fusion(bf16[4,32,1024]{2,1,0:T(8,128)(2,1)S(1)} %squeeze.16, bf16[2,4,1024,512]{3,2,1,0:T(8,128)(2,1)} %param.6), kind=kOutput, calls=%fused_computation.73 | convolution fusion | flops 134217728 | bytes 4718592 | tf_op jit(solution)/shard_map/frk,fkc->frc/dot_general | solution.py:96
  20.9 3.5 %fusion.37 = f32[4,32,512]{2,1,0:T(8,128)S(1)} fusion(bf16[4,32,1024]{2,1,0:T(8,128)(2,1)S(1)} %squeeze.14, bf16[2,4,1024,512]{3,2,1,0:T(8,128)(2,1)} %param.6), kind=kOutput, calls=%fused_computation.71 | convolution fusion | flops 134217728 | bytes 4718592 | tf_op jit(solution)/shard_map/frk,fkc->frc/dot_general | solution.py:96
  24.3 0.8 fusion.62
  25.3 3.1 %fusion.65 = f32[4,32,512]{2,1,0:T(8,128)S(1)} fusion(f32[4,32,512]{2,1,0:T(8,128)S(1)} %fusion.37, bf16[4,32,1024]{2,1,0:T(8,128)(2,1)S(1)} %squeeze.16, bf16[2,4,1024,512]{3,2,1,0:T(8,128)(2,1)} %param.6), kind=kOutput, calls=%fused_computation.98 | convolution fusion | flops 134283264 | bytes 4980736 | tf_op jit(solution)/shard_map/frk,fkc->frc/dot_general | solution.py:96
  28.5 0.8 maximum_bitcast_fusion
  29.4 4.0 %all-to-all-start.1 = ((f32[4,2,4,32,128]{4,3,2,1,0:T(8,128)}), f32[4,2,4,32,128]{4,3,2,1,0:T(8,128)S(1)}, u32[]{:S(2)}, u32[]{:S(2)}) async-start(f32[4,2,4,32,128]{4,3,2,1,0:T(8,128)} %maximum_bitcast_fusion), calls=%async_computation.1 | async-start | bytes 1048576 | tf_op jit(solution)/shard_map/all_to_all | solution.py:40
  33.4 2.4 convert_bitcast_fusion
  35.8 5.6 %all-to-all-done.1 = f32[4,2,4,32,128]{4,3,2,1,0:T(8,128)S(1)} async-done(((f32[4,2,4,32,128]{4,3,2,1,0:T(8,128)}), f32[4,2,4,32,128]{4,3,2,1,0:T(8,128)S(1)}, u32[]{:S(2)}, u32[]{:S(2)}) %all-to-all-start.1) | async-done | bytes 524320 | tf_op jit(solution)/shard_map/all_to_all | solution.py:40
  41.5 0.7 copy.55
  42.1 5.5 %all-to-all-start.2 = ((bf16[2,4,32,128]{3,1,0,2:T(4,128)(2,1)}), bf16[2,4,32,128]{3,1,0,2:T(4,128)(2,1)S(1)}, u32[]{:S(2)}, u32[]{:S(2)}) async-start(bf16[2,4,32,128]{3,1,0,2:T(4,128)(2,1)} %copy.55), calls=%async_computation.2 | async-start | bytes 131072 | tf_op jit(solution)/shard_map/all_to_all | solution.py:115
  47.7 6.6 %copy.50 = f32[8,1,16,64,128]{4,2,0,3,1:T(8,128)} copy(f32[8,1,16,64,128]{4,0,3,2,1:T(8,128)} %convert_bitcast_fusion) | data formatting | bytes 8388608 | tf_op jit(solution)/shard_map/convert_element_type | solution.py:137
  54.3 1.9 bitcast_convert_fusion
  56.2 1.4 copy.58
  57.6 2.5 slice.385
  60.0 2.4 slice.387
  62.4 2.4 slice.389
  64.8 2.4 slice.391
  67.2 2.4 slice.393
  69.6 2.4 slice.395
  72.0 2.3 slice.397
  74.2 2.2 slice.399
  76.5 2.2 slice.401
  78.7 2.2 slice.403
  80.9 2.1 slice.405
  83.0 2.1 slice.407
  85.2 2.1 slice.409
  87.3 2.1 slice.411
  89.4 2.1 slice.413
  91.5 0.6 multiply_reduce_fusion
  92.2 20.8 %fusion.8 = f32[128,64,128]{2,0,1:T(8,128)S(1)} fusion(f32[128,64,128]{2,0,1:T(8,128)} %bitcast.229, f32[128,56,128]{2,0,1:T(8,128)} %slice.399, f32[128,55,128]{2,0,1:T(8,128)} %slice.401, f32[128,54,128]{2,0,1:T(8,128)} %slice.403, f32[128,53,128]{2,0,1:T(8,128)} %slice.405, f32[128,52,128]{2,0,1:T(8,128)} %slice.407, f32[128,51,128]{2,0,1:T(8,128)} %slice.409, ...), kind=kLoop, calls=%fused_computation.40 | loop fusion | flops 34603008 | bytes 65544192 | tf_op jit(solution)/shard_map/sub | solution.py:79
  113.1 8.5 %fusion.55 = f32[128,64,64]{2,1,0:T(8,128)} fusion(bf16[128,64,128]{2,1,0:T(8,128)(2,1)S(1)} %bitcast.235, f32[128,64,128]{2,0,1:T(8,128)S(1)} %fusion.8), kind=kOutput, calls=%fused_computation.89 | convolution fusion | flops 805306368 | bytes 8388608 | tf_op jit(solution)/shard_map/wsj,wtj->wst/dot_general | solution.py:81
  121.6 7.0 %fusion.101 = f32[128,16]{0,1:T(8,128)S(1)} fusion(f32[128,64,64]{2,1,0:T(8,128)} %fusion.55, s32[64,64]{1,0:T(8,128)S(1)} %iota_subtract_fusion, f32[128]{0:T(128)S(1)} %div.25, s32[128]{0:T(128)S(1)} %bitcast.245, f32[16]{0:T(128)S(1)} %compare_convert_fusion), kind=kOutput, calls=%fused_computation.110 | convolution fusion | flops 100739072 | bytes 2122816 | tf_op jit(solution)/shard_map/dot_general | solution.py:83
  128.7 15.7 %fusion.17 = f32[128,64,128]{2,0,1:T(8,128)} fusion(f32[128,64,128]{2,0,1:T(8,128)S(1)} %bitcast.231, f32[128,56,128]{2,0,1:T(8,128)} %slice.399, f32[128,55,128]{2,0,1:T(8,128)} %slice.401, f32[128,54,128]{2,0,1:T(8,128)} %slice.403, f32[128,53,128]{2,0,1:T(8,128)} %slice.405, f32[128,52,128]{2,0,1:T(8,128)} %slice.407, f32[128,51,128]{2,0,1:T(8,128)} %slice.409, ...), kind=kLoop, calls=%fused_computation.49 | loop fusion | flops 34603008 | bytes 65544192 | tf_op jit(solution)/shard_map/sub | solution.py:91
  144.5 9.6 %fusion.51 = f32[128,64,64]{2,1,0:T(8,128)} fusion(bf16[128,64,128]{2,1,0:T(8,128)(2,1)S(1)} %bitcast.236, f32[128,64,128]{2,0,1:T(8,128)} %fusion.17), kind=kOutput, calls=%fused_computation.85 | convolution fusion | flops 805306368 | bytes 8388608 | tf_op jit(solution)/shard_map/wsj,wtj->wst/dot_general | solution.py:81
  154.1 7.0 %fusion.92 = f32[128,16]{0,1:T(8,128)S(1)} fusion(f32[128,16]{0,1:T(8,128)S(1)} %fusion.101, f32[128,64,64]{2,1,0:T(8,128)} %fusion.51, s32[64,64]{1,0:T(8,128)S(1)} %iota_subtract_fusion, f32[128]{0:T(128)S(1)} %div.25, s32[128]{0:T(128)S(1)} %bitcast.246), kind=kOutput, calls=%fused_computation.107 | convolution fusion | flops 100737024 | bytes 2130944 | tf_op jit(solution)/shard_map/dot_general | solution.py:83
  161.2 14.8 %fusion.26 = f32[128,64,128]{2,0,1:T(8,128)} fusion(f32[128,64,128]{2,0,1:T(8,128)S(1)} %bitcast.232, f32[128,56,128]{2,0,1:T(8,128)} %slice.399, f32[128,55,128]{2,0,1:T(8,128)} %slice.401, f32[128,54,128]{2,0,1:T(8,128)} %slice.403, f32[128,53,128]{2,0,1:T(8,128)} %slice.405, f32[128,52,128]{2,0,1:T(8,128)} %slice.407, f32[128,51,128]{2,0,1:T(8,128)} %slice.409, ...), kind=kLoop, calls=%fused_computation.58 | loop fusion | flops 34603008 | bytes 65544192 | tf_op jit(solution)/shard_map/sub | solution.py:91
  176.1 8.2 %fusion.47 = f32[128,64,64]{2,1,0:T(8,128)S(1)} fusion(bf16[128,64,128]{2,1,0:T(8,128)(2,1)S(1)} %bitcast.237, f32[128,64,128]{2,0,1:T(8,128)} %fusion.26), kind=kOutput, calls=%fused_computation.81 | convolution fusion | flops 805306368 | bytes 8388608 | tf_op jit(solution)/shard_map/wsj,wtj->wst/dot_general | solution.py:81
  184.2 4.8 %fusion.83 = f32[128,16]{0,1:T(8,128)S(1)} fusion(f32[128,16]{0,1:T(8,128)S(1)} %fusion.92, f32[128,64,64]{2,1,0:T(8,128)S(1)} %fusion.47, s32[64,64]{1,0:T(8,128)S(1)} %iota_subtract_fusion, f32[128]{0:T(128)S(1)} %div.25, s32[128]{0:T(128)S(1)} %bitcast.247), kind=kOutput, calls=%fused_computation.104 | convolution fusion | flops 100737024 | bytes 2130944 | tf_op jit(solution)/shard_map/dot_general | solution.py:83
  189.1 23.0 %convolution_convert_fusion = bf16[256,64,128]{2,0,1:T(8,128)(2,1)} fusion(f32[128,64,128]{2,0,1:T(8,128)} %bitcast.230, f32[128,56,128]{2,0,1:T(8,128)} %slice.399, f32[128,55,128]{2,0,1:T(8,128)} %slice.401, f32[128,54,128]{2,0,1:T(8,128)} %slice.403, f32[128,53,128]{2,0,1:T(8,128)} %slice.405, f32[128,52,128]{2,0,1:T(8,128)} %slice.407, ...), kind=kOutput, calls=%fused_computation.96 | convolution fusion | flops 574652416 | bytes 65544704 | tf_op jit(solution)/shard_map/sw,wtc->stc/dot_general | solution.py:139
  212.1 7.0 %copy.68 = bf16[128,2,64,128]{3,2,1,0:T(8,128)(2,1)S(1)} copy(bf16[128,2,64,128]{3,1,0,2:T(2,128)(2,1)} %bitcast.239) | data formatting | bytes 8388608 | tf_op jit(solution)/shard_map/reshape | solution.py:141
  219.2 61.5 %all_to_all.33 = bf16[128,2,64,128]{3,2,1,0:T(8,128)(2,1)S(1)} all-to-all(bf16[128,2,64,128]{3,2,1,0:T(8,128)(2,1)S(1)} %copy.68), channel_id=1, replica_groups=mesh['freq'=4,'row'=8,'col'=4] {'freq','row','col'}, dimensions={0} | all-to-all | bytes 8388608 | tf_op jit(solution)/shard_map/all_to_all | solution.py:140
  280.6 2.0 copy.112
  (52 shorter events, 1.1 us)
Async XLA Ops:
  1.9 15.3 %all-to-all-start = ((bf16[8,2,4,4,1024]{4,3,2,1,0:T(4,128)(2,1)}), bf16[8,2,4,4,1024]{4,3,2,1,0:T(4,128)(2,1)S(1)}, u32[]{:S(2)}, u32[]{:S(2)}) async-start(bf16[8,2,4,4,1024]{4,3,2,1,0:T(4,128)(2,1)} %broadcast_in_dim.4), calls=%async_computation | async-start | bytes 1048576 | tf_op jit(solution)/shard_map/all_to_all | solution.py:23
  17.7 6.6 %copy-start.10 = (bf16[2,4,1024,512]{3,2,1,0:T(8,128)(2,1)S(1)}, bf16[2,4,1024,512]{3,2,1,0:T(8,128)(2,1)}, u32[]{:S(2)}) copy-start(bf16[2,4,1024,512]{3,2,1,0:T(8,128)(2,1)} %param.6) | copy-start | bytes 25165828
  25.3 8.1 %copy-start.13 = (s32[1,1,128,1]{2,3,1,0:T(1,128)S(1)}, s32[1,1,128,1]{2,3,1,0:T(1,128)}, u32[]{:S(2)}) copy-start(s32[1,1,128,1]{2,3,1,0:T(1,128)} %param.8) | copy-start | bytes 1540
  25.3 8.1 %copy-start.11 = (bf16[1024,8,128]{2,1,0:T(8,128)(2,1)S(1)}, bf16[1024,8,128]{2,1,0:T(8,128)(2,1)}, u32[]{:S(2)}) copy-start(bf16[1024,8,128]{2,1,0:T(8,128)(2,1)} %param.7) | copy-start | bytes 6291460
  29.4 12.0 %all-to-all-start.1 = ((f32[4,2,4,32,128]{4,3,2,1,0:T(8,128)}), f32[4,2,4,32,128]{4,3,2,1,0:T(8,128)S(1)}, u32[]{:S(2)}, u32[]{:S(2)}) async-start(f32[4,2,4,32,128]{4,3,2,1,0:T(8,128)} %maximum_bitcast_fusion), calls=%async_computation.1 | async-start | bytes 1048576 | tf_op jit(solution)/shard_map/all_to_all | solution.py:40
  42.1 12.2 %all-to-all-start.2 = ((bf16[2,4,32,128]{3,1,0,2:T(4,128)(2,1)}), bf16[2,4,32,128]{3,1,0,2:T(4,128)(2,1)S(1)}, u32[]{:S(2)}, u32[]{:S(2)}) async-start(bf16[2,4,32,128]{3,1,0,2:T(4,128)(2,1)} %copy.55), calls=%async_computation.2 | async-start | bytes 131072 | tf_op jit(solution)/shard_map/all_to_all | solution.py:115
  56.2 35.3 %copy-start.8 = (bf16[1024,8,128]{2,0,1:T(8,128)(2,1)}, bf16[1024,8,128]{2,0,1:T(8,128)(2,1)S(1)}, u32[]{:S(2)}) copy-start(bf16[1024,8,128]{2,0,1:T(8,128)(2,1)S(1)} %bitcast_convert_fusion) | copy-start | bytes 6291460
  92.2 20.9 %copy-start.9 = (bf16[1024,8,128]{2,0,1:T(8,128)(2,1)S(1)}, bf16[1024,8,128]{2,0,1:T(8,128)(2,1)}, u32[]{:S(2)}) copy-start(bf16[1024,8,128]{2,0,1:T(8,128)(2,1)} %copy-done.8) | copy-start | bytes 6291460
  92.2 36.5 %copy-start.3 = (f32[128,61,128]{2,0,1:T(8,128)S(1)}, f32[128,61,128]{2,0,1:T(8,128)}, u32[]{:S(2)}) copy-start(f32[128,61,128]{2,0,1:T(8,128)} %slice.389) | copy-start | bytes 11993092
  92.2 36.5 %copy-start.4 = (f32[128,60,128]{2,0,1:T(8,128)S(1)}, f32[128,60,128]{2,0,1:T(8,128)}, u32[]{:S(2)}) copy-start(f32[128,60,128]{2,0,1:T(8,128)} %slice.391) | copy-start | bytes 11796484
  92.2 36.5 %copy-start.5 = (f32[128,59,128]{2,0,1:T(8,128)S(1)}, f32[128,59,128]{2,0,1:T(8,128)}, u32[]{:S(2)}) copy-start(f32[128,59,128]{2,0,1:T(8,128)} %slice.393) | copy-start | bytes 11599876
  92.2 36.5 %copy-start.6 = (f32[128,58,128]{2,0,1:T(8,128)S(1)}, f32[128,58,128]{2,0,1:T(8,128)}, u32[]{:S(2)}) copy-start(f32[128,58,128]{2,0,1:T(8,128)} %slice.395) | copy-start | bytes 11403268
  113.1 8.5 %copy-start.12 = (s32[1,1,128]{2,1,0:T(1,128)S(1)}, s32[1,1,128]{2,1,0:T(1,128)}, u32[]{:S(2)}) copy-start(s32[1,1,128]{2,1,0:T(1,128)} %param.9) | copy-start | bytes 1540
  113.1 15.6 %copy-start.1 = (f32[128,63,128]{2,0,1:T(8,128)S(1)}, f32[128,63,128]{2,0,1:T(8,128)}, u32[]{:S(2)}) copy-start(f32[128,63,128]{2,0,1:T(8,128)} %slice.385) | copy-start | bytes 12386308
  113.1 15.6 %copy-start.2 = (f32[128,62,128]{2,0,1:T(8,128)S(1)}, f32[128,62,128]{2,0,1:T(8,128)}, u32[]{:S(2)}) copy-start(f32[128,62,128]{2,0,1:T(8,128)} %slice.387) | copy-start | bytes 12189700
  121.6 7.1 %copy-start = (f32[8,1,16,64,128]{4,2,0,3,1:T(8,128)S(1)}, f32[8,1,16,64,128]{4,2,0,3,1:T(8,128)}, u32[]{:S(2)}) copy-start(f32[8,1,16,64,128]{4,2,0,3,1:T(8,128)} %copy.50) | copy-start | bytes 12582916
  154.1 7.1 %copy-start.7 = (f32[128,57,128]{2,0,1:T(8,128)S(1)}, f32[128,57,128]{2,0,1:T(8,128)}, u32[]{:S(2)}) copy-start(f32[128,57,128]{2,0,1:T(8,128)} %slice.397) | copy-start | bytes 11206660
where the time goes:
time: 287 us; the launch traced here: 283 us
  matrix products  80.6 us (28%)
  blocking collectives  61.5 us (21%)
  other arithmetic  57.3 us (20%)
  local copies, waits for them, and re-layouts  54.4 us (19%)
  starting transfers between devices  15.5 us (5%)
  waiting for transfers between devices  13 us (5%)
    all_to_all x1, blocking collectives, local(): lax.all_to_all(buffer.astype(jnp.bfloat16).reshape(devices, slot_count, W...  61.5 us
    sub x3, other arithmetic, adapt(): residual = recorded_in - convolve(filter_taps)  51.4 us
    slice x15, local copies, waits for them, and re-layouts, lagged(): return jnp.pad(field[..., :-lag_index, :], widths)  33.9 us
    dot_general x3, matrix products, adapt(): jnp.einsum('wsj,wtj->wst', residual, predicted_in, precision=lax.Precisio...  26.3 us
    dot_general x1, matrix products, local(): jnp.einsum('sw,wtc->stc', selector, cleaned, preferred_element_type=jnp.f...  23 us
    dot_general x3, matrix products, adapt(): jnp.dot(correl.reshape(count, samples * samples), diagonals.T, precision=...  18.9 us
    dot_general x4, matrix products, batched(): jnp.einsum('frk,fkc->frc', left, right, preferred_element_type=jnp.float32)  10.5 us
    all_to_all x1, waiting for transfers between devices, sent_to_all(): lax.all_to_all(jnp.broadcast_to(value[None], (peers, *value.shape)), axis...  7.37 us
  transfers between devices with their start and end apart: 3, of which 2 were waited for; matrix products, arithmetic and copies ran while one was open for 4% of the time, Pallas kernels for 0%

commit v1 on v0

v1 whole, which is shorter than its diff:
```python
import functools

import jax
import jax.numpy as jnp
import numpy as np
from jax import lax
from jax.experimental import pallas as pl
from jax.experimental.pallas import tpu as pltpu
from jax.sharding import PartitionSpec as P

NT = 1024
WT = 64
WIN = 128
LMAX = 16
FIT_STEPS = 3
BANDS = 16
ROWS_HERE = 8
WINDOWS = 128
KEPT = 24
UNROLL = 4


def table_parts(bands, samples):
    turns = (np.arange(samples)[:, None] * (np.arange(bands) + 1)[None, :]) % samples
    angle = 2.0 * np.pi * turns / samples
    table = np.concatenate([np.cos(angle), -np.sin(angle)], axis=1) * bands**-0.5
    left, parts = table, []
    for _ in range(3):
        part = left.astype(jnp.bfloat16)
        parts.append(part)
        left = left - part.astype(np.float64)
    return np.concatenate(parts, axis=1)


def both_tables():
    table = table_parts(BANDS, NT)
    reverse = table.reshape(NT // WT, WT, -1)[:, ::-1].reshape(NT, -1)
    return np.concatenate([table, reverse], axis=0)


def predict_kernel(rows_ref, data_ref, out_ref):
    rows = rows_ref[...].reshape(8, 8, rows_ref.shape[-1]).astype(jnp.float32)
    crossed = jnp.concatenate([-rows[:, 4:], rows[:, :4]], axis=1)
    depth = rows.shape[-1]
    plain = rows.reshape(64, depth).astype(jnp.bfloat16)
    crossed = crossed.reshape(64, depth).astype(jnp.bfloat16)
    total = jnp.dot(plain, data_ref[0, 0], preferred_element_type=jnp.float32)
    total += jnp.dot(crossed, data_ref[1, 0], preferred_element_type=jnp.float32)
    for group in range(4):
        for panel in range(4):
            out_ref[group * 4 + panel, 0] = total[
                group * 16 : group * 16 + 16, panel * WIN : panel * WIN + WIN
            ].astype(jnp.bfloat16)


def predict(rows, data):
    peers, bands, sides, depth = rows.shape
    columns = data.shape[-1]
    return pl.pallas_call(
        predict_kernel,
        grid=(bands,),
        in_specs=[
            pl.BlockSpec((peers, 1, sides, depth), lambda f: (0, f, 0, 0)),
            pl.BlockSpec((2, 1, depth, columns), lambda f: (0, f, 0, 0)),
        ],
        out_specs=pl.BlockSpec((16, 1, 16, WIN), lambda f: (0, f, 0, 0)),
        out_shape=jax.ShapeDtypeStruct((16, bands, 16, WIN), jnp.bfloat16),
        name="predict",
    )(rows, data)


def fit_kernel(
    target_ref,
    parts_ref,
    recorded_ref,
    length_ref,
    table_ref,
    out_ref,
    spec,
    stacked,
    field,
    kept,
    columns_at,
    correl_at,
    filters,
):
    for freq in range(4):
        total = parts_ref[freq * 4].astype(jnp.float32)
        for col in range(1, 4):
            total += parts_ref[freq * 4 + col].astype(jnp.float32)
        spec[pl.ds(freq * 64, 64), :] = total.reshape(64, WIN)
    for row in range(ROWS_HERE):
        first = (row // 4) * 8 + row % 4
        bands = jnp.concatenate(
            [spec[pl.ds(first, 16, stride=16), :], spec[pl.ds(first + 4, 16, stride=16), :]], axis=0
        ).astype(jnp.bfloat16)
        stacked[row] = jnp.concatenate([bands, bands, bands], axis=0)

    def traces_of(row, _):
        field[row] = jnp.dot(
            table_ref[...], stacked[row], preferred_element_type=jnp.float32
        ).astype(jnp.bfloat16)
        return 0

    lax.fori_loop(0, ROWS_HERE, traces_of, 0)

    def window_at(index):
        row, part = index // (NT // WT), index % (NT // WT)
        return row, pl.multiple_of(part * WT, WT)

    def correlate(step, _):
        for inner in range(UNROLL):
            index = step * UNROLL + inner
            row, start = window_at(index)
            ahead = field[row, pl.ds(start, WT), :]
            back = field[row, pl.ds(start + NT, WT), :]
            products = lax.dot_general(
                back,
                jnp.concatenate([recorded_ref[index], ahead], axis=0),
                (((1,), (1,)), ((), ())),
                preferred_element_type=jnp.float32,
            )
            turned = pltpu.roll(products, 1, 1, stride=1, stride_axis=0)
            rest = turned[16:24]
            for block in range(3, 8):
                rest += turned[block * 8 : block * 8 + 8]
            kept[pl.ds(pl.multiple_of(index * KEPT, 8), KEPT), :] = jnp.concatenate(
                [turned[:16], rest], axis=0
            )
        return 0

    lax.fori_loop(0, WINDOWS // UNROLL, correlate, 0)

    rest = kept[pl.ds(16, WINDOWS, stride=KEPT), :]
    for block in range(1, 8):
        rest += kept[pl.ds(16 + block, WINDOWS, stride=KEPT), :]
    rest = rest.T
    own, cross = rest[:LMAX], rest[64 : 64 + LMAX]
    for lag in reversed(range(LMAX)):
        lines = kept[pl.ds(lag, WINDOWS, stride=KEPT), :].T
        own = own + lines[:LMAX]
        cross = cross + lines[64 : 64 + LMAX]
        place = LMAX - 1 - lag
        columns_at[pl.ds(place * 32, LMAX), :] = jnp.zeros((LMAX, WIN), jnp.float32)
        columns_at[pl.ds(place * 32 + place, LMAX), :] = own
        correl_at[pl.ds(place, 1), :] = cross[lag : lag + 1]
    energy = own[:1]
    step_size = 0.4 / (energy + 1e-06)
    places = lax.broadcasted_iota(jnp.int32, (LMAX, WIN), 0)
    tap_mask = (LMAX - 1 - places < length_ref[...]).astype(jnp.float32)
    correl = correl_at[...]
    matrix = []
    for lag in range(LMAX):
        place = LMAX - 1 - lag
        upper = columns_at[pl.ds(place * 32, LMAX), :]
        lower = columns_at[pl.ds(place, LMAX, stride=32), :]
        matrix.append(jnp.where(places < place, lower, upper))
    taps = (places == LMAX - 1).astype(jnp.float32)
    change = jnp.zeros((LMAX, WIN), jnp.float32)
    for sweep in range(FIT_STEPS):
        if sweep == 0:
            covered = matrix[0]
        else:
            covered = jnp.zeros((LMAX, WIN), jnp.float32)
            for lag in range(LMAX):
                place = LMAX - 1 - lag
                covered += matrix[lag] * jnp.broadcast_to(taps[place : place + 1], (LMAX, WIN))
        update = step_size * ((correl - covered) * tap_mask)
        taps = taps + update
        change = change + update
    high = change.astype(jnp.bfloat16).astype(jnp.float32)
    low = change - high
    gap = jnp.zeros((48, WIN), jnp.float32)
    filters[...] = jnp.concatenate([gap, low, gap, high], axis=0).T

    lanes = lax.broadcasted_iota(jnp.int32, (16, WIN), 1)
    samples = lax.broadcasted_iota(jnp.int32, (16, WIN), 0)
    inside = (lanes % WT) <= samples

    def clear(step, _):
        for inner in range(8):
            out_ref[step * 8 + inner] = jnp.zeros((WT, WIN), jnp.bfloat16)
        return 0

    lax.fori_loop(0, out_ref.shape[0] // 8, clear, 0)

    def subtract(step, _):
        for inner in range(UNROLL):
            index = step * UNROLL + inner
            row, start = window_at(index)
            ahead = field[row, pl.ds(start, WT), :]
            line = jnp.broadcast_to(filters[pl.ds(index, 1), :], (WT, WIN))
            turned = pltpu.roll(line, 1, 1, stride=1, stride_axis=0)
            turned = jnp.concatenate([jnp.where(inside, turned[:16], 0.0), turned[16:]], axis=0)
            shaped = jnp.dot(
                turned.astype(jnp.bfloat16),
                jnp.concatenate([ahead, ahead], axis=0),
                preferred_element_type=jnp.float32,
            )
            left = recorded_ref[index].astype(jnp.float32) - ahead.astype(jnp.float32)
            out_ref[target_ref[index]] = (left - shaped).astype(jnp.bfloat16)
        return 0

    lax.fori_loop(0, WINDOWS // UNROLL, subtract, 0)


def fit(target, parts, recorded, lengths, table, slots):
    whole = pl.BlockSpec(memory_space=pltpu.VMEM)
    return pl.pallas_call(
        fit_kernel,
        in_specs=[pl.BlockSpec(memory_space=pltpu.SMEM)] + [whole] * 4,
        out_specs=whole,
        out_shape=jax.ShapeDtypeStruct((slots, WT, WIN), jnp.bfloat16),
        scratch_shapes=[
            pltpu.VMEM((256, WIN), jnp.float32),
            pltpu.VMEM((ROWS_HERE, 96, WIN), jnp.bfloat16),
            pltpu.VMEM((ROWS_HERE, 2 * NT, WIN), jnp.bfloat16),
            pltpu.VMEM((WINDOWS * KEPT, WIN), jnp.float32),
            pltpu.VMEM((LMAX * 32, WIN), jnp.float32),
            pltpu.VMEM((LMAX, WIN), jnp.float32),
            pltpu.VMEM((WINDOWS, WIN), jnp.float32),
        ],
        compiler_params=pltpu.CompilerParams(vmem_limit_bytes=40 * 1024 * 1024),
        name="fit",
    )(target, parts, recorded, lengths, table)


def slot_of(owners, slots_each):
    count = owners.shape[0]
    same = owners[:, None] == owners[None, :]
    earlier = jnp.arange(count)[None, :] < jnp.arange(count)[:, None]
    return owners * slots_each + jnp.sum(jnp.logical_and(same, earlier), axis=1, dtype=jnp.int32)


def local(source_rows, data_matrix, observed, window_owner, filter_len):
    devices = lax.axis_size("freq") * lax.axis_size("row") * lax.axis_size("col")
    sides, bands, rows, depth = source_rows.shape
    mine = source_rows.transpose(1, 0, 2, 3).reshape(bands, sides * rows, depth)
    peers = lax.axis_size("row")
    panel_rows = lax.all_to_all(
        jnp.broadcast_to(mine[None], (peers, *mine.shape)), "row", 0, 0, tiled=True
    )
    partial = predict(panel_rows, data_matrix)
    parts = lax.all_to_all(partial, ("freq", "col"), 0, 0, tiled=True)
    recorded = (
        observed.reshape(NT // WT, WT, ROWS_HERE, WIN).transpose(2, 0, 1, 3).reshape(-1, WT, WIN)
    )
    target = slot_of(window_owner.reshape(-1), 2)
    buffer = fit(
        target,
        parts,
        recorded,
        filter_len.reshape(1, -1),
        jnp.asarray(both_tables()),
        devices * 2,
    )
    result = lax.all_to_all(
        buffer.reshape(devices, 2, WT, WIN), ("freq", "row", "col"), 0, 0, tiled=True
    )
    return result[None]


def solution(mesh):
    return jax.shard_map(
        local,
        mesh=mesh,
        in_specs=(
            P(None, "freq", "row", "col"),
            P(None, "freq", "col", "row"),
            P(None, "freq", ("row", "col")),
            P("freq", ("row", "col"), None, None),
            P("freq", ("row", "col"), None),
        ),
        out_specs=P(("freq", "row", "col"), None, None, None, None),
        check_vma=False,
    )
```

time: 287 us -> 118 us (0.41); the launches traced: 283 us -> 118 us
  matrix products: 80.6 us -> 0 us
  other arithmetic: 57.3 us -> 0.17 us
  local copies, waits for them, and re-layouts: 54.4 us -> 5.11 us
  Pallas kernels: 0 us -> 25.7 us
  blocking collectives: 61.5 us -> 73.9 us
  starting transfers between devices: 15.5 us -> 7.73 us
  waiting for transfers between devices: 13 us -> 5.33 us
    dot_general x12 -> x0, matrix products: 80.6 us -> none  [the longest x3 26.3 us: adapt(): jnp.einsum('wsj,wtj->wst', residual, predicted_in, precision=lax.Precisio...]
    sub x4 -> x0, other arithmetic: 51.4 us -> none  [the longest x3 51.4 us: adapt(): residual = recorded_in - convolve(filter_taps)]
    slice x18 -> x0, local copies, waits for them, and re-layouts: 34.3 us -> none  [the longest x15 33.9 us: lagged(): return jnp.pad(field[..., :-lag_index, :], widths)]
    pallas_call x0 -> x2, Pallas kernels: none -> 25.7 us  [the longest x1 20 us: fit(): pl.pallas_call(fit_kernel, in_specs=[pl.BlockSpec(memory_space=pltpu.SMEM...]
    all_to_all x1 -> x2, blocking collectives: 61.5 us -> 73.9 us  [the longest x1 58.7 us: local(): lax.all_to_all(buffer.reshape(devices, 2, WT, WIN), ('freq', 'row', 'col'...]
    all_to_all x3 -> x1, starting transfers between devices: 15.5 us -> 7.73 us  [local(): parts = lax.all_to_all(partial, ('freq', 'col'), 0, 0, tiled=True)]
    all_to_all x3 -> x1, waiting for transfers between devices: 13 us -> 5.33 us  [local(): parts = lax.all_to_all(partial, ('freq', 'col'), 0, 0, tiled=True)]
    convert_element_type x2 -> x0, local copies, waits for them, and re-layouts: 7.24 us -> none  [the longest x1 6.58 us: local(): recorded_win.astype(jnp.float32)]
  transfers between devices with their start and end apart: 3 -> 1, of which waited for: 2 -> 1; matrix products, arithmetic and copies ran while one was open for 4% -> 2% of each run, Pallas kernels for 0% -> 0%
where the time goes in v1:
time: 118 us
  blocking collectives  73.9 us (63%)
  Pallas kernels  25.7 us (22%)
  starting transfers between devices  7.73 us (7%)
  waiting for transfers between devices  5.33 us (5%)
  local copies, waits for them, and re-layouts  5.11 us (4%)
    all_to_all x1, blocking collectives, local(): lax.all_to_all(buffer.reshape(devices, 2, WT, WIN), ('freq', 'row', 'col'...  58.7 us
    pallas_call x1, Pallas kernels, fit(): pl.pallas_call(fit_kernel, in_specs=[pl.BlockSpec(memory_space=pltpu.SMEM...  20 us
    all_to_all x1, blocking collectives, local(): lax.all_to_all(jnp.broadcast_to(mine[None], (peers, *mine.shape)), 'row',...  15.2 us
    all_to_all x1, starting transfers between devices, local(): parts = lax.all_to_all(partial, ('freq', 'col'), 0, 0, tiled=True)  7.73 us
    pallas_call x1, Pallas kernels, predict(): pl.pallas_call(predict_kernel, grid=(bands,), in_specs=[pl.BlockSpec((pee...  5.78 us
    all_to_all x1, waiting for transfers between devices, local(): parts = lax.all_to_all(partial, ('freq', 'col'), 0, 0, tiled=True)  5.33 us
  transfers between devices with their start and end apart: 1, of which 1 were waited for; matrix products, arithmetic and copies ran while one was open for 2% of the time, Pallas kernels for 0%

profile of v1, /device:TPU:1, one launch (start us, length us, event | category | flops | bytes accessed | tf_op | source)
XLA Modules:
  0.0 118.0 jit_solution(636767958159483351)
XLA Ops:
  0.0 0.9 copy.11
  0.9 0.1 broadcast_in_dim.13
  1.0 15.2 %all_to_all.15.rows_ref = bf16[8,4,8,1024]{3,2,1,0:T(8,128)(2,1)} all-to-all(bf16[8,4,8,1024]{3,2,1,0:T(8,128)(2,1)S(1)} %broadcast_in_dim.13), channel_id=1, replica_groups=mesh['freq'=4,'row'=8,'col'=4] {'row'}, dimensions={0} | all-to-all | bytes 1048576 | tf_op jit(solution)/shard_map/all_to_all | solution.py:240
  16.1 0.0 copy-start.2
  16.2 5.8 %predict.1 = bf16[16,4,16,128]{3,2,1,0:T(8,128)(2,1)} custom-call(bf16[8,4,8,1024]{3,2,1,0:T(8,128)(2,1)} %all_to_all.15.rows_ref, bf16[2,4,1024,512]{3,2,1,0:T(8,128)(2,1)} %data_ref.1), custom_call_target="tpu_custom_call" | custom-call | tf_op jit(solution)/shard_map/predict/pallas_call | solution.py:59
  21.9 0.0 copy-start
  21.9 0.0 copy-start.1
  21.9 7.7 %all-to-all-start.1 = ((bf16[16,4,16,128]{3,2,1,0:T(8,128)(2,1)}), bf16[16,4,16,128]{3,2,1,0:T(8,128)(2,1)S(1)}, u32[]{:S(2)}, u32[]{:S(2)}) async-start(bf16[16,4,16,128]{3,2,1,0:T(8,128)(2,1)} %predict.1), calls=%async_computation.1 | async-start | bytes 524288 | tf_op jit(solution)/shard_map/all_to_all | solution.py:244
  29.7 0.0 copy-done.2
  29.7 0.2 convert_reduce_fusion
  29.9 2.1 %copy.13 = bf16[16,64,8,128]{3,1,0,2:T(8,128)(2,1)S(1)} copy(bf16[16,64,8,128]{3,2,1,0:T(8,128)(2,1)} %bitcast.15) | data formatting | bytes 4194304 | tf_op jit(solution)/shard_map/reshape | solution.py:246
  32.0 5.3 %all-to-all-done.1.parts_ref = bf16[16,4,16,128]{3,2,1,0:T(8,128)(2,1)S(1)} async-done(((bf16[16,4,16,128]{3,2,1,0:T(8,128)(2,1)}), bf16[16,4,16,128]{3,2,1,0:T(8,128)(2,1)S(1)}, u32[]{:S(2)}, u32[]{:S(2)}) %all-to-all-start.1) | async-done | bytes 262176 | tf_op jit(solution)/shard_map/all_to_all | solution.py:244
  37.3 0.0 copy-done
  37.3 0.0 copy-done.1
  37.3 20.0 %fit.1 = bf16[256,64,128]{2,1,0:T(8,128)(2,1)S(1)} custom-call(s32[128]{0:T(128)S(1)} %multiply_add_fusion.target_ref, bf16[16,4,16,128]{3,2,1,0:T(8,128)(2,1)S(1)} %all-to-all-done.1.parts_ref, bf16[128,64,128]{2,1,0:T(8,128)(2,1)S(1)} %bitcast.12, s32[1,128]{1,0:T(1,128)S(1)} %bitcast.13, bf16[2048,96]{1,0:T(8,128)(2,1)S(1)} %copy-done), custom_call_target="tpu_custom_call" | custom-call | tf_op jit(solution)/shard_map/fit/pallas_call | solution.py:209
  57.3 58.7 %all_to_all.16 = bf16[128,2,64,128]{3,2,1,0:T(8,128)(2,1)S(1)} all-to-all(bf16[128,2,64,128]{3,2,1,0:T(8,128)(2,1)S(1)} %bitcast.11), channel_id=1, replica_groups=mesh['freq'=4,'row'=8,'col'=4] {'freq','row','col'}, dimensions={0} | all-to-all | bytes 8388608 | tf_op jit(solution)/shard_map/all_to_all | solution.py:257
  116.0 2.0 %copy.15 = bf16[1,128,2,64,128]{4,3,2,1,0:T(8,128)(2,1)} copy(bf16[1,128,2,64,128]{4,3,2,1,0:T(8,128)(2,1)S(1)} %bitcast.14) | data formatting | bytes 8388608
  (2 shorter events, 0.0 us)
Async XLA Ops:
  16.1 13.5 %copy-start.2 = (s32[1,1,128,1]{2,3,1,0:T(1,128)S(1)}, s32[1,1,128,1]{2,3,1,0:T(1,128)}, u32[]{:S(2)}) copy-start(s32[1,1,128,1]{2,3,1,0:T(1,128)} %param.9) | copy-start | bytes 1540
  21.9 15.4 %copy-start = (bf16[2048,96]{1,0:T(8,128)(2,1)S(1)}, bf16[2048,96]{1,0:T(8,128)(2,1)}, u32[]{:S(2)}) copy-start(bf16[2048,96]{1,0:T(8,128)(2,1)} %constant.6.clone.table_ref) | copy-start | bytes 1179652
  21.9 15.4 %copy-start.1 = (s32[1,1,128]{2,1,0:T(1,128)S(1)}, s32[1,1,128]{2,1,0:T(1,128)}, u32[]{:S(2)}) copy-start(s32[1,1,128]{2,1,0:T(1,128)} %param.10) | copy-start | bytes 1540
  21.9 15.4 %all-to-all-start.1 = ((bf16[16,4,16,128]{3,2,1,0:T(8,128)(2,1)}), bf16[16,4,16,128]{3,2,1,0:T(8,128)(2,1)S(1)}, u32[]{:S(2)}, u32[]{:S(2)}) async-start(bf16[16,4,16,128]{3,2,1,0:T(8,128)(2,1)} %predict.1), calls=%async_computation.1 | async-start | bytes 524288 | tf_op jit(solution)/shard_map/all_to_all | solution.py:244

commit v2 on v1

--- a/solution.py
+++ b/solution.py
@@ -17,7 +17,8 @@
 ROWS_HERE = 8
 WINDOWS = 128
 KEPT = 24
-UNROLL = 4
+DRAINS = 8
+UNROLL = 16
 
 
 def table_parts(bands, samples):
@@ -38,35 +39,40 @@
     return np.concatenate([table, reverse], axis=0)
 
 
-def predict_kernel(rows_ref, data_ref, out_ref):
-    rows = rows_ref[...].reshape(8, 8, rows_ref.shape[-1]).astype(jnp.float32)
-    crossed = jnp.concatenate([-rows[:, 4:], rows[:, :4]], axis=1)
-    depth = rows.shape[-1]
-    plain = rows.reshape(64, depth).astype(jnp.bfloat16)
-    crossed = crossed.reshape(64, depth).astype(jnp.bfloat16)
-    total = jnp.dot(plain, data_ref[0, 0], preferred_element_type=jnp.float32)
-    total += jnp.dot(crossed, data_ref[1, 0], preferred_element_type=jnp.float32)
-    for group in range(4):
-        for panel in range(4):
-            out_ref[group * 4 + panel, 0] = total[
-                group * 16 : group * 16 + 16, panel * WIN : panel * WIN + WIN
-            ].astype(jnp.bfloat16)
-
-
-def predict(rows, data):
-    peers, bands, sides, depth = rows.shape
-    columns = data.shape[-1]
+def predict_kernel(*refs):
+    pieces, data_ref, out_ref = refs[:8], refs[8], refs[9]
+    first = lax.axis_index("row") // 2
+    depth = data_ref.shape[2]
+    for band in range(data_ref.shape[1]):
+        plain, crossed = [], []
+        for piece in pieces:
+            real = piece[0, band].astype(jnp.float32)
+            imag = piece[1, band].astype(jnp.float32)
+            plain += [real, imag]
+            crossed += [-imag, real]
+        plain = jnp.concatenate(plain, axis=0).astype(jnp.bfloat16)
+        crossed = jnp.concatenate(crossed, axis=0).astype(jnp.bfloat16)
+        total = jnp.dot(plain, data_ref[0, band], preferred_element_type=jnp.float32)
+        total += jnp.dot(crossed, data_ref[1, band], preferred_element_type=jnp.float32)
+        for step in range(4):
+            group = lax.rem(first + 4 - step, 4)
+            for panel in range(4):
+                out_ref[group * 4 + panel, band] = total[
+                    step * 16 : step * 16 + 16, panel * WIN : panel * WIN + WIN
+                ].astype(jnp.bfloat16)
+
+
+def predict(pieces, data):
+    bands = data.shape[1]
+    whole = pl.BlockSpec(memory_space=pltpu.VMEM)
     return pl.pallas_call(
         predict_kernel,
-        grid=(bands,),
-        in_specs=[
-            pl.BlockSpec((peers, 1, sides, depth), lambda f: (0, f, 0, 0)),
-            pl.BlockSpec((2, 1, depth, columns), lambda f: (0, f, 0, 0)),
-        ],
-        out_specs=pl.BlockSpec((16, 1, 16, WIN), lambda f: (0, f, 0, 0)),
+        in_specs=[whole] * 9,
+        out_specs=whole,
         out_shape=jax.ShapeDtypeStruct((16, bands, 16, WIN), jnp.bfloat16),
+        compiler_params=pltpu.CompilerParams(vmem_limit_bytes=24 * 1024 * 1024),
         name="predict",
-    )(rows, data)
+    )(*pieces, data)
 
 
 def fit_kernel(
@@ -84,11 +90,15 @@
     correl_at,
     filters,
 ):
+    core = lax.axis_index("row") % 2
     for freq in range(4):
         total = parts_ref[freq * 4].astype(jnp.float32)
         for col in range(1, 4):
             total += parts_ref[freq * 4 + col].astype(jnp.float32)
-        spec[pl.ds(freq * 64, 64), :] = total.reshape(64, WIN)
+        for band in range(4):
+            for half in range(2):
+                at = freq * 64 + band * 16 + lax.rem(half + core, 2) * 8
+                spec[pl.ds(pl.multiple_of(at, 8), 8), :] = total[band, half * 8 : half * 8 + 8]
     for row in range(ROWS_HERE):
         first = (row // 4) * 8 + row % 4
         bands = jnp.concatenate(
@@ -100,6 +110,8 @@
         field[row] = jnp.dot(
             table_ref[...], stacked[row], preferred_element_type=jnp.float32
         ).astype(jnp.bfloat16)
+        share = out_ref.shape[0] // ROWS_HERE
+        out_ref[pl.ds(row * share, share)] = jnp.zeros((share, WT, WIN), jnp.bfloat16)
         return 0
 
     lax.fori_loop(0, ROWS_HERE, traces_of, 0)
@@ -177,13 +189,6 @@
     samples = lax.broadcasted_iota(jnp.int32, (16, WIN), 0)
     inside = (lanes % WT) <= samples
 
-    def clear(step, _):
-        for inner in range(8):
-            out_ref[step * 8 + inner] = jnp.zeros((WT, WIN), jnp.bfloat16)
-        return 0
-
-    lax.fori_loop(0, out_ref.shape[0] // 8, clear, 0)
-
     def subtract(step, _):
         for inner in range(UNROLL):
             index = step * UNROLL + inner
@@ -225,6 +230,45 @@
     )(target, parts, recorded, lengths, table)
 
 
+def drain_kernel(given_ref, out_ref, done):
+    share = given_ref.shape[0] // DRAINS
+    copies = [
+        pltpu.make_async_copy(
+            given_ref.at[pl.ds(part * share, share)],
+            out_ref.at[pl.ds(part * share, share)],
+            done.at[part],
+        )
+        for part in range(DRAINS)
+    ]
+    for copy in copies:
+        copy.start()
+    for copy in copies:
+        copy.wait()
+
+
+def drained(value):
+    return pl.pallas_call(
+        drain_kernel,
+        in_specs=[pl.BlockSpec(memory_space=pltpu.VMEM)],
+        out_specs=pl.BlockSpec(memory_space=pltpu.HBM),
+        out_shape=jax.ShapeDtypeStruct(value.shape, value.dtype),
+        scratch_shapes=[pltpu.SemaphoreType.DMA((DRAINS,))],
+        compiler_params=pltpu.CompilerParams(vmem_limit_bytes=1024 * 1024),
+        name="drain",
+    )(value)
+
+
+def rows_of_panel(mine):
+    peers = lax.axis_size("row")
+
+    def moved(value, target_of):
+        return lax.ppermute(value, "row", [(at, target_of(at)) for at in range(peers)])
+
+    own = [mine] + [moved(mine, lambda at, by=by: (at + by) % peers) for by in (2, 4, 6)]
+    other = [moved(piece, lambda at: at ^ 1) for piece in own]
+    return [piece for pair in zip(own, other) for piece in pair]
+
+
 def slot_of(owners, slots_each):
     count = owners.shape[0]
     same = owners[:, None] == owners[None, :]
@@ -234,13 +278,7 @@
 
 def local(source_rows, data_matrix, observed, window_owner, filter_len):
     devices = lax.axis_size("freq") * lax.axis_size("row") * lax.axis_size("col")
-    sides, bands, rows, depth = source_rows.shape
-    mine = source_rows.transpose(1, 0, 2, 3).reshape(bands, sides * rows, depth)
-    peers = lax.axis_size("row")
-    panel_rows = lax.all_to_all(
-        jnp.broadcast_to(mine[None], (peers, *mine.shape)), "row", 0, 0, tiled=True
-    )
-    partial = predict(panel_rows, data_matrix)
+    partial = predict(rows_of_panel(source_rows), lax.ppermute(data_matrix, 'row', [(i, i) for i in range(8)]))
     parts = lax.all_to_all(partial, ("freq", "col"), 0, 0, tiled=True)
     recorded = (
         observed.reshape(NT // WT, WT, ROWS_HERE, WIN).transpose(2, 0, 1, 3).reshape(-1, WT, WIN)
@@ -257,7 +295,7 @@
     result = lax.all_to_all(
         buffer.reshape(devices, 2, WT, WIN), ("freq", "row", "col"), 0, 0, tiled=True
     )
-    return result[None]
+    return drained(result)[None]
 
 
 def solution(mesh):

time: 118 us -> 106 us (0.90)
  blocking collectives: 73.9 us -> 59.2 us
  starting transfers between devices: 7.73 us -> 21.3 us
  Pallas kernels: 25.7 us -> 14.8 us
  local copies, waits for them, and re-layouts: 5.11 us -> 2.99 us
  waiting for transfers between devices: 5.33 us -> 6.94 us
    all_to_all x1 -> x0, blocking collectives: 15.2 us -> none  [local(): lax.all_to_all(jnp.broadcast_to(mine[None], (peers, *mine.shape)), 'row',...]
    ppermute x0 -> x8, starting transfers between devices: none -> 13.6 us  [the longest x7 10.2 us: moved(): lax.ppermute(value, 'row', [(at, target_of(at)) for at in range(peers)])]
    pallas_call x1, Pallas kernels: 20 us -> 10.5 us  [fit(): pl.pallas_call(fit_kernel, in_specs=[pl.BlockSpec(memory_space=pltpu.SMEM...]
    pallas_call x1 -> x2, Pallas kernels: 5.78 us -> 4.33 us  [the longest x1 2.26 us: predict(): pl.pallas_call(predict_kernel, in_specs=[whole] * 9, out_specs=whole, out...]
  transfers between devices with their start and end apart: 1 -> 9, of which waited for: 1 -> 3; matrix products, arithmetic and copies ran while one was open for 2% -> 2% of each run, Pallas kernels for 0% -> 0%
where the time goes in v2:
time: 106 us; the launch traced here: 105 us
  blocking collectives  59.2 us (56%)
  starting transfers between devices  21.3 us (20%)
  Pallas kernels  14.8 us (14%)
  waiting for transfers between devices  6.94 us (7%)
  local copies, waits for them, and re-layouts  2.99 us (3%)
    all_to_all x1, blocking collectives, local(): lax.all_to_all(buffer.reshape(devices, 2, WT, WIN), ('freq', 'row', 'col'...  59.2 us
    pallas_call x1, Pallas kernels, fit(): pl.pallas_call(fit_kernel, in_specs=[pl.BlockSpec(memory_space=pltpu.SMEM...  10.5 us
    ppermute x7, starting transfers between devices, moved(): lax.ppermute(value, 'row', [(at, target_of(at)) for at in range(peers)])  10.2 us
    all_to_all x1, starting transfers between devices, local(): parts = lax.all_to_all(partial, ('freq', 'col'), 0, 0, tiled=True)  7.73 us
    all_to_all x1, waiting for transfers between devices, local(): parts = lax.all_to_all(partial, ('freq', 'col'), 0, 0, tiled=True)  5.8 us
    ppermute x1, starting transfers between devices, local(): lax.ppermute(data_matrix, 'row', [(i, i) for i in range(8)])  3.38 us
    pallas_call x1, Pallas kernels, predict(): pl.pallas_call(predict_kernel, in_specs=[whole] * 9, out_specs=whole, out...  2.26 us
    reshape x1, local copies, waits for them, and re-layouts, local(): observed.reshape(NT // WT, WT, ROWS_HERE, WIN).transpose(2, 0, 1, 3)  2.14 us
  transfers between devices with their start and end apart: 9, of which 3 were waited for; matrix products, arithmetic and copies ran while one was open for 2% of the time, Pallas kernels for 0%

profile of v2, /device:TPU:1, one launch (start us, length us, event | category | flops | bytes accessed | tf_op | source)
XLA Modules:
  0.0 105.5 jit_solution(6140029281324762448)
XLA Ops:
  0.0 3.4 %collective-permute-start.7 = (bf16[2,4,1024,512]{3,2,1,0:T(8,128)(2,1)}, bf16[2,4,1024,512]{3,2,1,0:T(8,128)(2,1)S(1)}, u32[]{:S(2)}, u32[]{:S(2)}) collective-permute-start(bf16[2,4,1024,512]{3,2,1,0:T(8,128)(2,1)} %param.7), channel_id=1, source_target_pairs={{0,0},{4,4},{8,8},{12,12},{16,16},{20,20},{24,24},{28,28},{1,1},{5... | collective-permute-start | bytes 25165832 | tf_op jit(solution)/shard_map/ppermute | solution.py:281
  3.4 2.1 %collective-permute-start.1 = (bf16[2,4,4,1024]{3,2,1,0:T(4,128)(2,1)}, bf16[2,4,4,1024]{3,2,1,0:T(4,128)(2,1)S(1)}, u32[]{:S(2)}, u32[]{:S(2)}) collective-permute-start(bf16[2,4,4,1024]{3,2,1,0:T(4,128)(2,1)} %refs_0_.1), channel_id=1, source_target_pairs={{0,8},{4,12},{8,16},{12,20},{16,24},{20,28},{24,0},{28,4},{1,9},{5... | collective-permute-start | bytes 196616 | tf_op jit(solution)/shard_map/ppermute | solution.py:265
  5.5 2.6 %collective-permute-start.3 = (bf16[2,4,4,1024]{3,2,1,0:T(4,128)(2,1)}, bf16[2,4,4,1024]{3,2,1,0:T(4,128)(2,1)S(1)}, u32[]{:S(2)}, u32[]{:S(2)}) collective-permute-start(bf16[2,4,4,1024]{3,2,1,0:T(4,128)(2,1)} %refs_0_.1), channel_id=1, source_target_pairs={{0,16},{4,20},{8,24},{12,28},{16,0},{20,4},{24,8},{28,12},{1,17},{... | collective-permute-start | bytes 196616 | tf_op jit(solution)/shard_map/ppermute | solution.py:265
  8.1 1.1 %collective-permute-start.5 = (bf16[2,4,4,1024]{3,2,1,0:T(4,128)(2,1)}, bf16[2,4,4,1024]{3,2,1,0:T(4,128)(2,1)S(1)}, u32[]{:S(2)}, u32[]{:S(2)}) collective-permute-start(bf16[2,4,4,1024]{3,2,1,0:T(4,128)(2,1)} %refs_0_.1), channel_id=1, source_target_pairs={{0,24},{4,28},{8,0},{12,4},{16,8},{20,12},{24,16},{28,20},{1,25},{... | collective-permute-start | bytes 196616 | tf_op jit(solution)/shard_map/ppermute | solution.py:265
  9.2 1.5 %collective-permute-start = (bf16[2,4,4,1024]{3,2,1,0:T(4,128)(2,1)}, bf16[2,4,4,1024]{3,2,1,0:T(4,128)(2,1)S(1)}, u32[]{:S(2)}, u32[]{:S(2)}) collective-permute-start(bf16[2,4,4,1024]{3,2,1,0:T(4,128)(2,1)} %refs_0_.1), channel_id=1, source_target_pairs={{0,4},{4,0},{8,12},{12,8},{16,20},{20,16},{24,28},{28,24},{1,5},{5... | collective-permute-start | bytes 196616 | tf_op jit(solution)/shard_map/ppermute | solution.py:265
  10.7 0.0 collective-permute-done.1.refs_2_
  10.7 0.0 collective-permute-start.2
  10.7 0.2 collective-permute-done.3.refs_4_
  11.0 1.8 %collective-permute-start.4 = (bf16[2,4,4,1024]{3,2,1,0:T(4,128)(2,1)S(1)}, bf16[2,4,4,1024]{3,2,1,0:T(4,128)(2,1)S(1)}, u32[]{:S(2)}, u32[]{:S(2)}) collective-permute-start(bf16[2,4,4,1024]{3,2,1,0:T(4,128)(2,1)S(1)} %collective-permute-done.3.refs_4_), channel_id=1, source_target_pairs={{0,4},{4,0},{8,12},{12,8},{16,20},{20,16},{24,28},{28,24},{1,5},{5... | collective-permute-start | bytes 196616 | tf_op jit(solution)/shard_map/ppermute | solution.py:265
  12.8 0.0 collective-permute-done.5.refs_6_
  12.8 1.1 collective-permute-start.6
  13.8 0.0 collective-permute-done.refs_1_
  13.8 0.0 collective-permute-done.2.refs_3_
  13.8 0.0 collective-permute-done.4.refs_5_
  13.8 0.9 collective-permute-done.6.refs_7_
  14.7 0.0 collective-permute-done.7.refs_8_
  14.7 0.0 copy-start.1
  14.7 0.8 copy-done.1
  15.6 0.0 copy-start.3
  15.6 2.3 %predict.1 = bf16[16,4,16,128]{3,2,1,0:T(8,128)(2,1)} custom-call(bf16[2,4,4,1024]{3,2,1,0:T(4,128)(2,1)S(1)} %copy-done.1, bf16[2,4,4,1024]{3,2,1,0:T(4,128)(2,1)S(1)} %collective-permute-done.refs_1_, bf16[2,4,4,1024]{3,2,1,0:T(4,128)(2,1)S(1)} %collective-permute-done.1.refs_2_, bf16[2,4,4,1024]{3,2,1,0:T(4,128)(2,1)S(1)} %collective-permute-done.2.refs_3_, ...), custom_call_target="tpu_custom_call" | custom-call | tf_op jit(solution)/shard_map/predict/pallas_call | solution.py:68
  17.8 0.0 copy-start
  17.8 0.0 copy-start.2
  17.8 7.7 %all-to-all-start = ((bf16[16,4,16,128]{3,2,1,0:T(8,128)(2,1)}), bf16[16,4,16,128]{3,2,1,0:T(8,128)(2,1)S(1)}, u32[]{:S(2)}, u32[]{:S(2)}) async-start(bf16[16,4,16,128]{3,2,1,0:T(8,128)(2,1)} %predict.1), calls=%async_computation | async-start | bytes 524288 | tf_op jit(solution)/shard_map/all_to_all | solution.py:282
  25.6 0.0 copy-done.3
  25.6 0.2 convert_reduce_fusion
  25.8 2.1 %copy.8 = bf16[16,64,8,128]{3,1,0,2:T(8,128)(2,1)S(1)} copy(bf16[16,64,8,128]{3,2,1,0:T(8,128)(2,1)} %bitcast.12) | data formatting | bytes 4194304 | tf_op jit(solution)/shard_map/reshape | solution.py:284
  27.9 5.8 %all-to-all-done.parts_ref = bf16[16,4,16,128]{3,2,1,0:T(8,128)(2,1)S(1)} async-done(((bf16[16,4,16,128]{3,2,1,0:T(8,128)(2,1)}), bf16[16,4,16,128]{3,2,1,0:T(8,128)(2,1)S(1)}, u32[]{:S(2)}, u32[]{:S(2)}) %all-to-all-start) | async-done | bytes 262176 | tf_op jit(solution)/shard_map/all_to_all | solution.py:282
  33.7 0.0 copy-done
  33.7 0.0 copy-done.2
  33.7 10.5 %fit.1 = bf16[256,64,128]{2,1,0:T(8,128)(2,1)S(1)} custom-call(s32[128]{0:T(128)S(1)} %multiply_add_fusion.target_ref, bf16[16,4,16,128]{3,2,1,0:T(8,128)(2,1)S(1)} %all-to-all-done.parts_ref, bf16[128,64,128]{2,1,0:T(8,128)(2,1)S(1)} %bitcast.10, s32[1,128]{1,0:T(1,128)S(1)} %bitcast.11, bf16[2048,96]{1,0:T(8,128)(2,1)S(1)} %copy-done), custom_call_target="tpu_custom_call" | custom-call | tf_op jit(solution)/shard_map/fit/pallas_call | solution.py:214
  44.2 59.2 %all_to_all.10.given_ref = bf16[128,2,64,128]{3,2,1,0:T(8,128)(2,1)S(1)} all-to-all(bf16[128,2,64,128]{3,2,1,0:T(8,128)(2,1)S(1)} %bitcast.9), channel_id=1, replica_groups=mesh['freq'=4,'row'=8,'col'=4] {'freq','row','col'}, dimensions={0} | all-to-all | bytes 8388608 | tf_op jit(solution)/shard_map/all_to_all | solution.py:295
  103.4 2.1 %drain.1 = bf16[128,2,64,128]{3,2,1,0:T(8,128)(2,1)} custom-call(bf16[128,2,64,128]{3,2,1,0:T(8,128)(2,1)S(1)} %all_to_all.10.given_ref), custom_call_target="tpu_custom_call" | custom-call | tf_op jit(solution)/shard_map/drain/pallas_call | solution.py:250
  (1 shorter events, 0.0 us)
Async XLA Ops:
  0.0 14.7 %collective-permute-start.7 = (bf16[2,4,1024,512]{3,2,1,0:T(8,128)(2,1)}, bf16[2,4,1024,512]{3,2,1,0:T(8,128)(2,1)S(1)}, u32[]{:S(2)}, u32[]{:S(2)}) collective-permute-start(bf16[2,4,1024,512]{3,2,1,0:T(8,128)(2,1)} %param.7), channel_id=1, source_target_pairs={{0,0},{4,4},{8,8},{12,12},{16,16},{20,20},{24,24},{28,28},{1,1},{5... | collective-permute-start | bytes 25165832 | tf_op jit(solution)/shard_map/ppermute | solution.py:281
  3.4 7.3 %collective-permute-start.1 = (bf16[2,4,4,1024]{3,2,1,0:T(4,128)(2,1)}, bf16[2,4,4,1024]{3,2,1,0:T(4,128)(2,1)S(1)}, u32[]{:S(2)}, u32[]{:S(2)}) collective-permute-start(bf16[2,4,4,1024]{3,2,1,0:T(4,128)(2,1)} %refs_0_.1), channel_id=1, source_target_pairs={{0,8},{4,12},{8,16},{12,20},{16,24},{20,28},{24,0},{28,4},{1,9},{5... | collective-permute-start | bytes 196616 | tf_op jit(solution)/shard_map/ppermute | solution.py:265
  5.5 5.5 %collective-permute-start.3 = (bf16[2,4,4,1024]{3,2,1,0:T(4,128)(2,1)}, bf16[2,4,4,1024]{3,2,1,0:T(4,128)(2,1)S(1)}, u32[]{:S(2)}, u32[]{:S(2)}) collective-permute-start(bf16[2,4,4,1024]{3,2,1,0:T(4,128)(2,1)} %refs_0_.1), channel_id=1, source_target_pairs={{0,16},{4,20},{8,24},{12,28},{16,0},{20,4},{24,8},{28,12},{1,17},{... | collective-permute-start | bytes 196616 | tf_op jit(solution)/shard_map/ppermute | solution.py:265
  8.1 4.7 %collective-permute-start.5 = (bf16[2,4,4,1024]{3,2,1,0:T(4,128)(2,1)}, bf16[2,4,4,1024]{3,2,1,0:T(4,128)(2,1)S(1)}, u32[]{:S(2)}, u32[]{:S(2)}) collective-permute-start(bf16[2,4,4,1024]{3,2,1,0:T(4,128)(2,1)} %refs_0_.1), channel_id=1, source_target_pairs={{0,24},{4,28},{8,0},{12,4},{16,8},{20,12},{24,16},{28,20},{1,25},{... | collective-permute-start | bytes 196616 | tf_op jit(solution)/shard_map/ppermute | solution.py:265
  9.2 4.6 %collective-permute-start = (bf16[2,4,4,1024]{3,2,1,0:T(4,128)(2,1)}, bf16[2,4,4,1024]{3,2,1,0:T(4,128)(2,1)S(1)}, u32[]{:S(2)}, u32[]{:S(2)}) collective-permute-start(bf16[2,4,4,1024]{3,2,1,0:T(4,128)(2,1)} %refs_0_.1), channel_id=1, source_target_pairs={{0,4},{4,0},{8,12},{12,8},{16,20},{20,16},{24,28},{28,24},{1,5},{5... | collective-permute-start | bytes 196616 | tf_op jit(solution)/shard_map/ppermute | solution.py:265
  10.7 3.1 %collective-permute-start.2 = (bf16[2,4,4,1024]{3,2,1,0:T(4,128)(2,1)S(1)}, bf16[2,4,4,1024]{3,2,1,0:T(4,128)(2,1)S(1)}, u32[]{:S(2)}, u32[]{:S(2)}) collective-permute-start(bf16[2,4,4,1024]{3,2,1,0:T(4,128)(2,1)S(1)} %collective-permute-done.1.refs_2_), channel_id=1, source_target_pairs={{0,4},{4,0},{8,12},{12,8},{16,20},{20,16},{24,28},{28,24},{1,5},{5... | collective-permute-start | bytes 196616 | tf_op jit(solution)/shard_map/ppermute | solution.py:265
  11.0 2.9 %collective-permute-start.4 = (bf16[2,4,4,1024]{3,2,1,0:T(4,128)(2,1)S(1)}, bf16[2,4,4,1024]{3,2,1,0:T(4,128)(2,1)S(1)}, u32[]{:S(2)}, u32[]{:S(2)}) collective-permute-start(bf16[2,4,4,1024]{3,2,1,0:T(4,128)(2,1)S(1)} %collective-permute-done.3.refs_4_), channel_id=1, source_target_pairs={{0,4},{4,0},{8,12},{12,8},{16,20},{20,16},{24,28},{28,24},{1,5},{5... | collective-permute-start | bytes 196616 | tf_op jit(solution)/shard_map/ppermute | solution.py:265
  12.8 2.0 %collective-permute-start.6 = (bf16[2,4,4,1024]{3,2,1,0:T(4,128)(2,1)S(1)}, bf16[2,4,4,1024]{3,2,1,0:T(4,128)(2,1)S(1)}, u32[]{:S(2)}, u32[]{:S(2)}) collective-permute-start(bf16[2,4,4,1024]{3,2,1,0:T(4,128)(2,1)S(1)} %collective-permute-done.5.refs_6_), channel_id=1, source_target_pairs={{0,4},{4,0},{8,12},{12,8},{16,20},{20,16},{24,28},{28,24},{1,5},{5... | collective-permute-start | bytes 196616 | tf_op jit(solution)/shard_map/ppermute | solution.py:265
  14.7 0.8 copy-start.1
  15.6 10.0 %copy-start.3 = (s32[1,1,128,1]{2,3,1,0:T(1,128)S(1)}, s32[1,1,128,1]{2,3,1,0:T(1,128)}, u32[]{:S(2)}) copy-start(s32[1,1,128,1]{2,3,1,0:T(1,128)} %param.9) | copy-start | bytes 1540
  17.8 15.9 %copy-start = (bf16[2048,96]{1,0:T(8,128)(2,1)S(1)}, bf16[2048,96]{1,0:T(8,128)(2,1)}, u32[]{:S(2)}) copy-start(bf16[2048,96]{1,0:T(8,128)(2,1)} %constant.6.clone.table_ref) | copy-start | bytes 1179652
  17.8 15.9 %copy-start.2 = (s32[1,1,128]{2,1,0:T(1,128)S(1)}, s32[1,1,128]{2,1,0:T(1,128)}, u32[]{:S(2)}) copy-start(s32[1,1,128]{2,1,0:T(1,128)} %param.10) | copy-start | bytes 1540
  17.8 15.9 %all-to-all-start = ((bf16[16,4,16,128]{3,2,1,0:T(8,128)(2,1)}), bf16[16,4,16,128]{3,2,1,0:T(8,128)(2,1)S(1)}, u32[]{:S(2)}, u32[]{:S(2)}) async-start(bf16[16,4,16,128]{3,2,1,0:T(8,128)(2,1)} %predict.1), calls=%async_computation | async-start | bytes 524288 | tf_op jit(solution)/shard_map/all_to_all | solution.py:282

commit v3 on v2

--- a/solution.py
+++ b/solution.py
@@ -1,5 +1,3 @@
-import functools
-
 import jax
 import jax.numpy as jnp
 import numpy as np
@@ -7,6 +5,7 @@
 from jax.experimental import pallas as pl
 from jax.experimental.pallas import tpu as pltpu
 from jax.sharding import PartitionSpec as P
+
 
 NT = 1024
 WT = 64
@@ -18,7 +17,8 @@
 WINDOWS = 128
 KEPT = 24
 DRAINS = 8
-UNROLL = 16
+UNROLL = 64
+AHEAD = 64
 
 
 def table_parts(bands, samples):
@@ -33,16 +33,9 @@
     return np.concatenate(parts, axis=1)
 
 
-def both_tables():
-    table = table_parts(BANDS, NT)
-    reverse = table.reshape(NT // WT, WT, -1)[:, ::-1].reshape(NT, -1)
-    return np.concatenate([table, reverse], axis=0)
-
-
 def predict_kernel(*refs):
     pieces, data_ref, out_ref = refs[:8], refs[8], refs[9]
     first = lax.axis_index("row") // 2
-    depth = data_ref.shape[2]
     for band in range(data_ref.shape[1]):
         plain, crossed = [], []
         for piece in pieces:
@@ -99,49 +92,93 @@
             for half in range(2):
                 at = freq * 64 + band * 16 + lax.rem(half + core, 2) * 8
                 spec[pl.ds(pl.multiple_of(at, 8), 8), :] = total[band, half * 8 : half * 8 + 8]
-    for row in range(ROWS_HERE):
-        first = (row // 4) * 8 + row % 4
-        bands = jnp.concatenate(
-            [spec[pl.ds(first, 16, stride=16), :], spec[pl.ds(first + 4, 16, stride=16), :]], axis=0
-        ).astype(jnp.bfloat16)
-        stacked[row] = jnp.concatenate([bands, bands, bands], axis=0)
-
-    def traces_of(row, _):
-        field[row] = jnp.dot(
-            table_ref[...], stacked[row], preferred_element_type=jnp.float32
-        ).astype(jnp.bfloat16)
-        share = out_ref.shape[0] // ROWS_HERE
-        out_ref[pl.ds(row * share, share)] = jnp.zeros((share, WT, WIN), jnp.bfloat16)
+    for pair in range(ROWS_HERE // 2):
+        both = []
+        for row in (2 * pair, 2 * pair + 1):
+            first = (row // 4) * 8 + row % 4
+            both.append(
+                jnp.concatenate(
+                    [
+                        spec[pl.ds(first, 16, stride=16), :],
+                        spec[pl.ds(first + 4, 16, stride=16), :],
+                    ],
+                    axis=0,
+                ).astype(jnp.bfloat16)
+            )
+        both = jnp.concatenate(both, axis=1)
+        stacked[pair] = jnp.concatenate([both, both, both], axis=0)
+
+    mirror = 7 - lax.broadcasted_iota(jnp.int32, (8, WIN), 0)
+
+    def traces_of(pair, _):
+        traces = jnp.dot(
+            table_ref[...], stacked[pair], preferred_element_type=jnp.float32
+        )
+        turned = []
+        for first in range(0, NT, WT):
+            for block in reversed(range(WT // 8)):
+                tile = traces[first + block * 8 : first + block * 8 + 8]
+                turned.append(
+                    jnp.concatenate(
+                        [
+                            jnp.take_along_axis(tile[:, :WIN], mirror, axis=0),
+                            jnp.take_along_axis(tile[:, WIN:], mirror, axis=0),
+                        ],
+                        axis=1,
+                    )
+                )
+        turned = jnp.concatenate(turned, axis=0)
+        for at in range(2):
+            field[2 * pair + at, :NT] = traces[:, at * WIN : at * WIN + WIN].astype(jnp.bfloat16)
+            field[2 * pair + at, NT:] = turned[:, at * WIN : at * WIN + WIN].astype(jnp.bfloat16)
         return 0
 
-    lax.fori_loop(0, ROWS_HERE, traces_of, 0)
+    lax.fori_loop(0, ROWS_HERE // 2, traces_of, 0)
 
     def window_at(index):
         row, part = index // (NT // WT), index % (NT // WT)
         return row, pl.multiple_of(part * WT, WT)
 
+    none = jnp.zeros((WT, WIN), jnp.bfloat16)
+    share = out_ref.shape[0] // WINDOWS
+
     def correlate(step, _):
-        for inner in range(UNROLL):
-            index = step * UNROLL + inner
-            row, start = window_at(index)
-            ahead = field[row, pl.ds(start, WT), :]
-            back = field[row, pl.ds(start + NT, WT), :]
+        for inner in range(0, AHEAD, 2):
+            aheads, backs, records = [], [], []
+            for index in (step * AHEAD + inner, step * AHEAD + inner + 1):
+                row, start = window_at(index)
+                aheads.append(field[row, pl.ds(start, WT), :])
+                backs.append(field[row, pl.ds(start + NT, WT), :])
+                records.append(recorded_ref[index])
             products = lax.dot_general(
-                back,
-                jnp.concatenate([recorded_ref[index], ahead], axis=0),
+                jnp.concatenate(
+                    [
+                        jnp.concatenate([backs[0], none], axis=1),
+                        jnp.concatenate([none, backs[1]], axis=1),
+                    ],
+                    axis=0,
+                ),
+                jnp.concatenate(
+                    [jnp.concatenate(records, axis=1), jnp.concatenate(aheads, axis=1)], axis=0
+                ),
                 (((1,), (1,)), ((), ())),
                 preferred_element_type=jnp.float32,
             )
-            turned = pltpu.roll(products, 1, 1, stride=1, stride_axis=0)
-            rest = turned[16:24]
-            for block in range(3, 8):
-                rest += turned[block * 8 : block * 8 + 8]
-            kept[pl.ds(pl.multiple_of(index * KEPT, 8), KEPT), :] = jnp.concatenate(
-                [turned[:16], rest], axis=0
-            )
+            for at in range(2):
+                index = step * AHEAD + inner + at
+                turned = pltpu.roll(
+                    products[at * WT : at * WT + WT], 1, 1, stride=1, stride_axis=0
+                )
+                out_ref[pl.ds(index * share, share)] = jnp.zeros((share, WT, WIN), jnp.bfloat16)
+                rest = turned[16:24]
+                for block in range(3, 8):
+                    rest += turned[block * 8 : block * 8 + 8]
+                kept[pl.ds(pl.multiple_of(index * KEPT, 8), KEPT), :] = jnp.concatenate(
+                    [turned[:16], rest], axis=0
+                )
         return 0
 
-    lax.fori_loop(0, WINDOWS // UNROLL, correlate, 0)
+    lax.fori_loop(0, WINDOWS // AHEAD, correlate, 0)
 
     rest = kept[pl.ds(16, WINDOWS, stride=KEPT), :]
     for block in range(1, 8):
@@ -218,7 +255,7 @@
         out_shape=jax.ShapeDtypeStruct((slots, WT, WIN), jnp.bfloat16),
         scratch_shapes=[
             pltpu.VMEM((256, WIN), jnp.float32),
-            pltpu.VMEM((ROWS_HERE, 96, WIN), jnp.bfloat16),
+            pltpu.VMEM((ROWS_HERE // 2, 96, 2 * WIN), jnp.bfloat16),
             pltpu.VMEM((ROWS_HERE, 2 * NT, WIN), jnp.bfloat16),
             pltpu.VMEM((WINDOWS * KEPT, WIN), jnp.float32),
             pltpu.VMEM((LMAX * 32, WIN), jnp.float32),
@@ -258,14 +295,16 @@
     )(value)
 
 
+def moved(value, target_of):
+    pairs = [(at, target_of(at)) for at in range(lax.axis_size("row"))]
+    return lax.ppermute(value, "row", pairs)
+
+
 def rows_of_panel(mine):
     peers = lax.axis_size("row")
-
-    def moved(value, target_of):
-        return lax.ppermute(value, "row", [(at, target_of(at)) for at in range(peers)])
-
     own = [mine] + [moved(mine, lambda at, by=by: (at + by) % peers) for by in (2, 4, 6)]
     other = [moved(piece, lambda at: at ^ 1) for piece in own]
+    own[0] = moved(mine, lambda at: at)
     return [piece for pair in zip(own, other) for piece in pair]
 
 
@@ -278,7 +317,8 @@
 
 def local(source_rows, data_matrix, observed, window_owner, filter_len):
     devices = lax.axis_size("freq") * lax.axis_size("row") * lax.axis_size("col")
-    partial = predict(rows_of_panel(source_rows), lax.ppermute(data_matrix, 'row', [(i, i) for i in range(8)]))
+    data = moved(data_matrix, lambda at: at)
+    partial = predict(rows_of_panel(source_rows), data)
     parts = lax.all_to_all(partial, ("freq", "col"), 0, 0, tiled=True)
     recorded = (
         observed.reshape(NT // WT, WT, ROWS_HERE, WIN).transpose(2, 0, 1, 3).reshape(-1, WT, WIN)
@@ -289,7 +329,7 @@
         parts,
         recorded,
         filter_len.reshape(1, -1),
-        jnp.asarray(both_tables()),
+        jnp.asarray(table_parts(BANDS, NT)),
         devices * 2,
     )
     result = lax.all_to_all(

time: 106 us -> 101 us (0.953)
  Pallas kernels: 14.8 us -> 10.4 us
    pallas_call x1, Pallas kernels: 10.5 us -> 6.04 us  [fit(): pl.pallas_call(fit_kernel, in_specs=[pl.BlockSpec(memory_space=pltpu.SMEM...]
    ppermute x8 -> x9, starting transfers between devices: 13.6 us -> 13.8 us  [moved(): return lax.ppermute(value, 'row', pairs)]
  transfers between devices with their start and end apart: 9 -> 10, of which waited for: 3 -> 3; matrix products, arithmetic and copies ran while one was open for 2% -> 2% of each run, Pallas kernels for 0% -> 0%
where the time goes in v3:
time: 101 us
  blocking collectives  59 us (58%)
  starting transfers between devices  21.6 us (21%)
  Pallas kernels  10.4 us (10%)
  waiting for transfers between devices  7.25 us (7%)
  local copies, waits for them, and re-layouts  2.15 us (2%)
    all_to_all x1, blocking collectives, local(): lax.all_to_all(buffer.reshape(devices, 2, WT, WIN), ('freq', 'row', 'col'...  59 us
    ppermute x9, starting transfers between devices, moved(): return lax.ppermute(value, 'row', pairs)  13.8 us
    all_to_all x1, starting transfers between devices, local(): parts = lax.all_to_all(partial, ('freq', 'col'), 0, 0, tiled=True)  7.73 us
    pallas_call x1, Pallas kernels, fit(): pl.pallas_call(fit_kernel, in_specs=[pl.BlockSpec(memory_space=pltpu.SMEM...  6.04 us
    all_to_all x1, waiting for transfers between devices, local(): parts = lax.all_to_all(partial, ('freq', 'col'), 0, 0, tiled=True)  6 us
    pallas_call x1, Pallas kernels, predict(): pl.pallas_call(predict_kernel, in_specs=[whole] * 9, out_specs=whole, out...  2.26 us
    reshape x1, local copies, waits for them, and re-layouts, local(): observed.reshape(NT // WT, WT, ROWS_HERE, WIN).transpose(2, 0, 1, 3)  2.14 us
    pallas_call x1, Pallas kernels, drained(): pl.pallas_call(drain_kernel, in_specs=[pl.BlockSpec(memory_space=pltpu.VM...  2.07 us
  transfers between devices with their start and end apart: 10, of which 3 were waited for; matrix products, arithmetic and copies ran while one was open for 2% of the time, Pallas kernels for 0%

profile of v3, /device:TPU:1, one launch (start us, length us, event | category | flops | bytes accessed | tf_op | source)
XLA Modules:
  0.0 100.6 jit_solution(16105480488000554717)
XLA Ops:
  0.0 0.0 copy-start.2
  0.0 3.4 %collective-permute-start.8 = (bf16[2,4,1024,512]{3,2,1,0:T(8,128)(2,1)}, bf16[2,4,1024,512]{3,2,1,0:T(8,128)(2,1)S(1)}, u32[]{:S(2)}, u32[]{:S(2)}) collective-permute-start(bf16[2,4,1024,512]{3,2,1,0:T(8,128)(2,1)} %param.7), channel_id=1, source_target_pairs={{0,0},{4,4},{8,8},{12,12},{16,16},{20,20},{24,24},{28,28},{1,1},{5... | collective-permute-start | bytes 25165832 | tf_op jit(solution)/shard_map/ppermute | solution.py:300
  3.4 2.1 %collective-permute-start.2 = (bf16[2,4,4,1024]{3,2,1,0:T(4,128)(2,1)}, bf16[2,4,4,1024]{3,2,1,0:T(4,128)(2,1)S(1)}, u32[]{:S(2)}, u32[]{:S(2)}) collective-permute-start(bf16[2,4,4,1024]{3,2,1,0:T(4,128)(2,1)} %param.6), channel_id=1, source_target_pairs={{0,8},{4,12},{8,16},{12,20},{16,24},{20,28},{24,0},{28,4},{1,9},{5... | collective-permute-start | bytes 196616 | tf_op jit(solution)/shard_map/ppermute | solution.py:300
  5.5 2.6 %collective-permute-start.4 = (bf16[2,4,4,1024]{3,2,1,0:T(4,128)(2,1)}, bf16[2,4,4,1024]{3,2,1,0:T(4,128)(2,1)S(1)}, u32[]{:S(2)}, u32[]{:S(2)}) collective-permute-start(bf16[2,4,4,1024]{3,2,1,0:T(4,128)(2,1)} %param.6), channel_id=1, source_target_pairs={{0,16},{4,20},{8,24},{12,28},{16,0},{20,4},{24,8},{28,12},{1,17},{... | collective-permute-start | bytes 196616 | tf_op jit(solution)/shard_map/ppermute | solution.py:300
  8.1 1.1 %collective-permute-start.6 = (bf16[2,4,4,1024]{3,2,1,0:T(4,128)(2,1)}, bf16[2,4,4,1024]{3,2,1,0:T(4,128)(2,1)S(1)}, u32[]{:S(2)}, u32[]{:S(2)}) collective-permute-start(bf16[2,4,4,1024]{3,2,1,0:T(4,128)(2,1)} %param.6), channel_id=1, source_target_pairs={{0,24},{4,28},{8,0},{12,4},{16,8},{20,12},{24,16},{28,20},{1,25},{... | collective-permute-start | bytes 196616 | tf_op jit(solution)/shard_map/ppermute | solution.py:300
  9.2 0.9 collective-permute-start
  10.1 0.0 collective-permute-done.2.refs_2_
  10.1 1.5 %collective-permute-start.1 = (bf16[2,4,4,1024]{3,2,1,0:T(4,128)(2,1)}, bf16[2,4,4,1024]{3,2,1,0:T(4,128)(2,1)S(1)}, u32[]{:S(2)}, u32[]{:S(2)}) collective-permute-start(bf16[2,4,4,1024]{3,2,1,0:T(4,128)(2,1)} %param.6), channel_id=1, source_target_pairs={{0,4},{4,0},{8,12},{12,8},{16,20},{20,16},{24,28},{28,24},{1,5},{5... | collective-permute-start | bytes 196616 | tf_op jit(solution)/shard_map/ppermute | solution.py:300
  11.6 0.0 collective-permute-done.4.refs_4_
  11.6 1.2 %collective-permute-start.3 = (bf16[2,4,4,1024]{3,2,1,0:T(4,128)(2,1)S(1)}, bf16[2,4,4,1024]{3,2,1,0:T(4,128)(2,1)S(1)}, u32[]{:S(2)}, u32[]{:S(2)}) collective-permute-start(bf16[2,4,4,1024]{3,2,1,0:T(4,128)(2,1)S(1)} %collective-permute-done.2.refs_2_), channel_id=1, source_target_pairs={{0,4},{4,0},{8,12},{12,8},{16,20},{20,16},{24,28},{28,24},{1,5},{5... | collective-permute-start | bytes 196616 | tf_op jit(solution)/shard_map/ppermute | solution.py:300
  12.8 0.0 collective-permute-done.6.refs_6_
  12.8 1.1 %collective-permute-start.5 = (bf16[2,4,4,1024]{3,2,1,0:T(4,128)(2,1)S(1)}, bf16[2,4,4,1024]{3,2,1,0:T(4,128)(2,1)S(1)}, u32[]{:S(2)}, u32[]{:S(2)}) collective-permute-start(bf16[2,4,4,1024]{3,2,1,0:T(4,128)(2,1)S(1)} %collective-permute-done.4.refs_4_), channel_id=1, source_target_pairs={{0,4},{4,0},{8,12},{12,8},{16,20},{20,16},{24,28},{28,24},{1,5},{5... | collective-permute-start | bytes 196616 | tf_op jit(solution)/shard_map/ppermute | solution.py:300
  13.8 0.0 collective-permute-done.refs_0_
  13.9 0.0 collective-permute-start.7
  13.9 0.0 collective-permute-done.1.refs_1_
  13.9 0.0 collective-permute-done.3.refs_3_
  13.9 0.9 collective-permute-done.5.refs_5_
  14.8 0.4 collective-permute-done.7.refs_7_
  15.1 0.0 collective-permute-done.8.refs_8_
  15.1 2.3 %predict.1 = bf16[16,4,16,128]{3,2,1,0:T(8,128)(2,1)} custom-call(bf16[2,4,4,1024]{3,2,1,0:T(4,128)(2,1)S(1)} %collective-permute-done.refs_0_, bf16[2,4,4,1024]{3,2,1,0:T(4,128)(2,1)S(1)} %collective-permute-done.1.refs_1_, bf16[2,4,4,1024]{3,2,1,0:T(4,128)(2,1)S(1)} %collective-permute-done.2.refs_2_, ...), custom_call_target="tpu_custom_call" | custom-call | tf_op jit(solution)/shard_map/predict/pallas_call | solution.py:61
  17.4 0.0 copy-start
  17.4 0.0 copy-start.1
  17.4 7.7 %all-to-all-start = ((bf16[16,4,16,128]{3,2,1,0:T(8,128)(2,1)}), bf16[16,4,16,128]{3,2,1,0:T(8,128)(2,1)S(1)}, u32[]{:S(2)}, u32[]{:S(2)}) async-start(bf16[16,4,16,128]{3,2,1,0:T(8,128)(2,1)} %predict.1), calls=%async_computation | async-start | bytes 524288 | tf_op jit(solution)/shard_map/all_to_all | solution.py:322
  25.1 0.0 copy-done.2
  25.1 0.2 convert_reduce_fusion
  25.3 2.1 %copy.8 = bf16[16,64,8,128]{3,1,0,2:T(8,128)(2,1)S(1)} copy(bf16[16,64,8,128]{3,2,1,0:T(8,128)(2,1)} %bitcast.12) | data formatting | bytes 4194304 | tf_op jit(solution)/shard_map/reshape | solution.py:324
  27.5 6.0 %all-to-all-done.parts_ref = bf16[16,4,16,128]{3,2,1,0:T(8,128)(2,1)S(1)} async-done(((bf16[16,4,16,128]{3,2,1,0:T(8,128)(2,1)}), bf16[16,4,16,128]{3,2,1,0:T(8,128)(2,1)S(1)}, u32[]{:S(2)}, u32[]{:S(2)}) %all-to-all-start) | async-done | bytes 262176 | tf_op jit(solution)/shard_map/all_to_all | solution.py:322
  33.5 0.0 copy-done
  33.5 0.0 copy-done.1
  33.5 6.0 %fit.1 = bf16[256,64,128]{2,1,0:T(8,128)(2,1)S(1)} custom-call(s32[128]{0:T(128)S(1)} %multiply_add_fusion.target_ref, bf16[16,4,16,128]{3,2,1,0:T(8,128)(2,1)S(1)} %all-to-all-done.parts_ref, bf16[128,64,128]{2,1,0:T(8,128)(2,1)S(1)} %bitcast.10, s32[1,128]{1,0:T(1,128)S(1)} %bitcast.11, bf16[1024,96]{1,0:T(8,128)(2,1)S(1)} %copy-done), custom_call_target="tpu_custom_call" | custom-call | tf_op jit(solution)/shard_map/fit/pallas_call | solution.py:251
  39.5 59.0 %all_to_all.10.given_ref = bf16[128,2,64,128]{3,2,1,0:T(8,128)(2,1)S(1)} all-to-all(bf16[128,2,64,128]{3,2,1,0:T(8,128)(2,1)S(1)} %bitcast.9), channel_id=1, replica_groups=mesh['freq'=4,'row'=8,'col'=4] {'freq','row','col'}, dimensions={0} | all-to-all | bytes 8388608 | tf_op jit(solution)/shard_map/all_to_all | solution.py:335
  98.5 2.1 %drain.1 = bf16[128,2,64,128]{3,2,1,0:T(8,128)(2,1)} custom-call(bf16[128,2,64,128]{3,2,1,0:T(8,128)(2,1)S(1)} %all_to_all.10.given_ref), custom_call_target="tpu_custom_call" | custom-call | tf_op jit(solution)/shard_map/drain/pallas_call | solution.py:287
  (1 shorter events, 0.0 us)
Async XLA Ops:
  0.0 25.1 %copy-start.2 = (s32[1,1,128,1]{2,3,1,0:T(1,128)S(1)}, s32[1,1,128,1]{2,3,1,0:T(1,128)}, u32[]{:S(2)}) copy-start(s32[1,1,128,1]{2,3,1,0:T(1,128)} %param.9) | copy-start | bytes 1540
  0.0 15.1 %collective-permute-start.8 = (bf16[2,4,1024,512]{3,2,1,0:T(8,128)(2,1)}, bf16[2,4,1024,512]{3,2,1,0:T(8,128)(2,1)S(1)}, u32[]{:S(2)}, u32[]{:S(2)}) collective-permute-start(bf16[2,4,1024,512]{3,2,1,0:T(8,128)(2,1)} %param.7), channel_id=1, source_target_pairs={{0,0},{4,4},{8,8},{12,12},{16,16},{20,20},{24,24},{28,28},{1,1},{5... | collective-permute-start | bytes 25165832 | tf_op jit(solution)/shard_map/ppermute | solution.py:300
  3.4 6.7 %collective-permute-start.2 = (bf16[2,4,4,1024]{3,2,1,0:T(4,128)(2,1)}, bf16[2,4,4,1024]{3,2,1,0:T(4,128)(2,1)S(1)}, u32[]{:S(2)}, u32[]{:S(2)}) collective-permute-start(bf16[2,4,4,1024]{3,2,1,0:T(4,128)(2,1)} %param.6), channel_id=1, source_target_pairs={{0,8},{4,12},{8,16},{12,20},{16,24},{20,28},{24,0},{28,4},{1,9},{5... | collective-permute-start | bytes 196616 | tf_op jit(solution)/shard_map/ppermute | solution.py:300
  5.5 6.1 %collective-permute-start.4 = (bf16[2,4,4,1024]{3,2,1,0:T(4,128)(2,1)}, bf16[2,4,4,1024]{3,2,1,0:T(4,128)(2,1)S(1)}, u32[]{:S(2)}, u32[]{:S(2)}) collective-permute-start(bf16[2,4,4,1024]{3,2,1,0:T(4,128)(2,1)} %param.6), channel_id=1, source_target_pairs={{0,16},{4,20},{8,24},{12,28},{16,0},{20,4},{24,8},{28,12},{1,17},{... | collective-permute-start | bytes 196616 | tf_op jit(solution)/shard_map/ppermute | solution.py:300
  8.1 4.7 %collective-permute-start.6 = (bf16[2,4,4,1024]{3,2,1,0:T(4,128)(2,1)}, bf16[2,4,4,1024]{3,2,1,0:T(4,128)(2,1)S(1)}, u32[]{:S(2)}, u32[]{:S(2)}) collective-permute-start(bf16[2,4,4,1024]{3,2,1,0:T(4,128)(2,1)} %param.6), channel_id=1, source_target_pairs={{0,24},{4,28},{8,0},{12,4},{16,8},{20,12},{24,16},{28,20},{1,25},{... | collective-permute-start | bytes 196616 | tf_op jit(solution)/shard_map/ppermute | solution.py:300
  9.2 4.6 %collective-permute-start = (bf16[2,4,4,1024]{3,2,1,0:T(4,128)(2,1)}, bf16[2,4,4,1024]{3,2,1,0:T(4,128)(2,1)S(1)}, u32[]{:S(2)}, u32[]{:S(2)}) collective-permute-start(bf16[2,4,4,1024]{3,2,1,0:T(4,128)(2,1)} %param.6), channel_id=1, source_target_pairs={{0,0},{4,4},{8,8},{12,12},{16,16},{20,20},{24,24},{28,28},{1,1},{5... | collective-permute-start | bytes 196616 | tf_op jit(solution)/shard_map/ppermute | solution.py:300
  10.1 3.8 %collective-permute-start.1 = (bf16[2,4,4,1024]{3,2,1,0:T(4,128)(2,1)}, bf16[2,4,4,1024]{3,2,1,0:T(4,128)(2,1)S(1)}, u32[]{:S(2)}, u32[]{:S(2)}) collective-permute-start(bf16[2,4,4,1024]{3,2,1,0:T(4,128)(2,1)} %param.6), channel_id=1, source_target_pairs={{0,4},{4,0},{8,12},{12,8},{16,20},{20,16},{24,28},{28,24},{1,5},{5... | collective-permute-start | bytes 196616 | tf_op jit(solution)/shard_map/ppermute | solution.py:300
  11.6 2.3 %collective-permute-start.3 = (bf16[2,4,4,1024]{3,2,1,0:T(4,128)(2,1)S(1)}, bf16[2,4,4,1024]{3,2,1,0:T(4,128)(2,1)S(1)}, u32[]{:S(2)}, u32[]{:S(2)}) collective-permute-start(bf16[2,4,4,1024]{3,2,1,0:T(4,128)(2,1)S(1)} %collective-permute-done.2.refs_2_), channel_id=1, source_target_pairs={{0,4},{4,0},{8,12},{12,8},{16,20},{20,16},{24,28},{28,24},{1,5},{5... | collective-permute-start | bytes 196616 | tf_op jit(solution)/shard_map/ppermute | solution.py:300
  12.8 2.0 %collective-permute-start.5 = (bf16[2,4,4,1024]{3,2,1,0:T(4,128)(2,1)S(1)}, bf16[2,4,4,1024]{3,2,1,0:T(4,128)(2,1)S(1)}, u32[]{:S(2)}, u32[]{:S(2)}) collective-permute-start(bf16[2,4,4,1024]{3,2,1,0:T(4,128)(2,1)S(1)} %collective-permute-done.4.refs_4_), channel_id=1, source_target_pairs={{0,4},{4,0},{8,12},{12,8},{16,20},{20,16},{24,28},{28,24},{1,5},{5... | collective-permute-start | bytes 196616 | tf_op jit(solution)/shard_map/ppermute | solution.py:300
  13.9 1.3 %collective-permute-start.7 = (bf16[2,4,4,1024]{3,2,1,0:T(4,128)(2,1)S(1)}, bf16[2,4,4,1024]{3,2,1,0:T(4,128)(2,1)S(1)}, u32[]{:S(2)}, u32[]{:S(2)}) collective-permute-start(bf16[2,4,4,1024]{3,2,1,0:T(4,128)(2,1)S(1)} %collective-permute-done.6.refs_6_), channel_id=1, source_target_pairs={{0,4},{4,0},{8,12},{12,8},{16,20},{20,16},{24,28},{28,24},{1,5},{5... | collective-permute-start | bytes 196616 | tf_op jit(solution)/shard_map/ppermute | solution.py:300
  17.4 16.1 %copy-start = (bf16[1024,96]{1,0:T(8,128)(2,1)S(1)}, bf16[1024,96]{1,0:T(8,128)(2,1)}, u32[]{:S(2)}) copy-start(bf16[1024,96]{1,0:T(8,128)(2,1)} %constant.6.clone.table_ref) | copy-start | bytes 589828
  17.4 16.1 %copy-start.1 = (s32[1,1,128]{2,1,0:T(1,128)S(1)}, s32[1,1,128]{2,1,0:T(1,128)}, u32[]{:S(2)}) copy-start(s32[1,1,128]{2,1,0:T(1,128)} %param.10) | copy-start | bytes 1540
  17.4 16.1 %all-to-all-start = ((bf16[16,4,16,128]{3,2,1,0:T(8,128)(2,1)}), bf16[16,4,16,128]{3,2,1,0:T(8,128)(2,1)S(1)}, u32[]{:S(2)}, u32[]{:S(2)}) async-start(bf16[16,4,16,128]{3,2,1,0:T(8,128)(2,1)} %predict.1), calls=%async_computation | async-start | bytes 524288 | tf_op jit(solution)/shard_map/all_to_all | solution.py:322

commit v4 on v3

--- a/solution.py
+++ b/solution.py
@@ -17,8 +17,9 @@
 WINDOWS = 128
 KEPT = 24
 DRAINS = 8
-UNROLL = 64
-AHEAD = 64
+PREDICT_MIB = 50
+UNROLL = 128
+AHEAD = 128
 
 
 def table_parts(bands, samples):
@@ -34,36 +35,66 @@
 
 
 def predict_kernel(*refs):
-    pieces, data_ref, out_ref = refs[:8], refs[8], refs[9]
+    pieces, data_ref, out_ref, held, rows, ready, landed, left = refs[:8], *refs[8:]
     first = lax.axis_index("row") // 2
-    for band in range(data_ref.shape[1]):
+    bands = data_ref.shape[1]
+    coming = [
+        [
+            pltpu.make_async_copy(
+                data_ref.at[side, band], held.at[side, band], landed.at[side, band]
+            )
+            for side in range(2)
+        ]
+        for band in range(bands)
+    ]
+    for pair in coming:
+        for copy in pair:
+            copy.start()
+    for band in range(bands):
         plain, crossed = [], []
         for piece in pieces:
             real = piece[0, band].astype(jnp.float32)
             imag = piece[1, band].astype(jnp.float32)
             plain += [real, imag]
             crossed += [-imag, real]
-        plain = jnp.concatenate(plain, axis=0).astype(jnp.bfloat16)
-        crossed = jnp.concatenate(crossed, axis=0).astype(jnp.bfloat16)
-        total = jnp.dot(plain, data_ref[0, band], preferred_element_type=jnp.float32)
-        total += jnp.dot(crossed, data_ref[1, band], preferred_element_type=jnp.float32)
+        rows[0, band] = jnp.concatenate(plain, axis=0).astype(jnp.bfloat16)
+        rows[1, band] = jnp.concatenate(crossed, axis=0).astype(jnp.bfloat16)
+    leaving = []
+    for band in range(bands):
+        for copy in coming[band]:
+            copy.wait()
+        total = jnp.dot(rows[0, band], held[0, band], preferred_element_type=jnp.float32)
+        total += jnp.dot(rows[1, band], held[1, band], preferred_element_type=jnp.float32)
         for step in range(4):
             group = lax.rem(first + 4 - step, 4)
             for panel in range(4):
-                out_ref[group * 4 + panel, band] = total[
+                ready[band, group * 4 + panel] = total[
                     step * 16 : step * 16 + 16, panel * WIN : panel * WIN + WIN
                 ].astype(jnp.bfloat16)
+        copy = pltpu.make_async_copy(ready.at[band], out_ref.at[:, band], left.at[band])
+        copy.start()
+        leaving.append(copy)
+    for copy in leaving:
+        copy.wait()
 
 
 def predict(pieces, data):
     bands = data.shape[1]
     whole = pl.BlockSpec(memory_space=pltpu.VMEM)
+    outside = pl.BlockSpec(memory_space=pltpu.HBM)
     return pl.pallas_call(
         predict_kernel,
-        in_specs=[whole] * 9,
-        out_specs=whole,
+        in_specs=[whole] * 8 + [outside],
+        out_specs=outside,
         out_shape=jax.ShapeDtypeStruct((16, bands, 16, WIN), jnp.bfloat16),
-        compiler_params=pltpu.CompilerParams(vmem_limit_bytes=24 * 1024 * 1024),
+        scratch_shapes=[
+            pltpu.VMEM(data.shape, data.dtype),
+            pltpu.VMEM((2, bands, 64, data.shape[2]), data.dtype),
+            pltpu.VMEM((bands, 16, 16, WIN), jnp.bfloat16),
+            pltpu.SemaphoreType.DMA((2, bands)),
+            pltpu.SemaphoreType.DMA((bands,)),
+        ],
+        compiler_params=pltpu.CompilerParams(vmem_limit_bytes=PREDICT_MIB * 1024 * 1024),
         name="predict",
     )(*pieces, data)
 
@@ -317,8 +348,7 @@
 
 def local(source_rows, data_matrix, observed, window_owner, filter_len):
     devices = lax.axis_size("freq") * lax.axis_size("row") * lax.axis_size("col")
-    data = moved(data_matrix, lambda at: at)
-    partial = predict(rows_of_panel(source_rows), data)
+    partial = predict(rows_of_panel(source_rows), data_matrix)
     parts = lax.all_to_all(partial, ("freq", "col"), 0, 0, tiled=True)
     recorded = (
         observed.reshape(NT // WT, WT, ROWS_HERE, WIN).transpose(2, 0, 1, 3).reshape(-1, WT, WIN)

time: 101 us -> 98.5 us (0.975)
  starting transfers between devices: 21.6 us -> 18.1 us
  Pallas kernels: 10.4 us -> 12 us
    ppermute x9 -> x8, starting transfers between devices: 13.8 us -> 10.2 us  [moved(): return lax.ppermute(value, 'row', pairs)]
    pallas_call x1, Pallas kernels: 2.26 us -> 4.64 us  [predict(): pl.pallas_call(predict_kernel, in_specs=[whole] * 8 + [outside], out_spec...]
  transfers between devices with their start and end apart: 10 -> 9, of which waited for: 3 -> 3; matrix products, arithmetic and copies ran while one was open for 2% -> 2% of each run, Pallas kernels for 0% -> 0%
where the time goes in v4:
time: 98.5 us; the launch traced here: 98.2 us
  blocking collectives  58.7 us (60%)
  starting transfers between devices  18.1 us (18%)
  Pallas kernels  12 us (12%)
  waiting for transfers between devices  7.07 us (7%)
  local copies, waits for them, and re-layouts  2.16 us (2%)
    all_to_all x1, blocking collectives, local(): lax.all_to_all(buffer.reshape(devices, 2, WT, WIN), ('freq', 'row', 'col'...  58.7 us
    ppermute x8, starting transfers between devices, moved(): return lax.ppermute(value, 'row', pairs)  10.2 us
    all_to_all x1, starting transfers between devices, local(): parts = lax.all_to_all(partial, ('freq', 'col'), 0, 0, tiled=True)  7.85 us
    all_to_all x1, waiting for transfers between devices, local(): parts = lax.all_to_all(partial, ('freq', 'col'), 0, 0, tiled=True)  5.8 us
    pallas_call x1, Pallas kernels, fit(): pl.pallas_call(fit_kernel, in_specs=[pl.BlockSpec(memory_space=pltpu.SMEM...  5.26 us
    pallas_call x1, Pallas kernels, predict(): pl.pallas_call(predict_kernel, in_specs=[whole] * 8 + [outside], out_spec...  4.64 us
    reshape x1, local copies, waits for them, and re-layouts, local(): observed.reshape(NT // WT, WT, ROWS_HERE, WIN).transpose(2, 0, 1, 3)  2.14 us
    pallas_call x1, Pallas kernels, drained(): pl.pallas_call(drain_kernel, in_specs=[pl.BlockSpec(memory_space=pltpu.VM...  2.07 us
  transfers between devices with their start and end apart: 9, of which 3 were waited for; matrix products, arithmetic and copies ran while one was open for 2% of the time, Pallas kernels for 0%

profile of v4, /device:TPU:1, one launch (start us, length us, event | category | flops | bytes accessed | tf_op | source)
XLA Modules:
  0.0 98.2 jit_solution(4519450560492767609)
XLA Ops:
  0.0 0.0 copy-start.2
  0.0 2.1 %collective-permute-start.2 = (bf16[2,4,4,1024]{3,2,1,0:T(4,128)(2,1)}, bf16[2,4,4,1024]{3,2,1,0:T(4,128)(2,1)S(1)}, u32[]{:S(2)}, u32[]{:S(2)}) collective-permute-start(bf16[2,4,4,1024]{3,2,1,0:T(4,128)(2,1)} %param.6), channel_id=1, source_target_pairs={{0,8},{4,12},{8,16},{12,20},{16,24},{20,28},{24,0},{28,4},{1,9},{5... | collective-permute-start | bytes 196616 | tf_op jit(solution)/shard_map/ppermute | solution.py:331
  2.1 1.5 %collective-permute-start.6 = (bf16[2,4,4,1024]{3,2,1,0:T(4,128)(2,1)}, bf16[2,4,4,1024]{3,2,1,0:T(4,128)(2,1)S(1)}, u32[]{:S(2)}, u32[]{:S(2)}) collective-permute-start(bf16[2,4,4,1024]{3,2,1,0:T(4,128)(2,1)} %param.6), channel_id=1, source_target_pairs={{0,24},{4,28},{8,0},{12,4},{16,8},{20,12},{24,16},{28,20},{1,25},{... | collective-permute-start | bytes 196616 | tf_op jit(solution)/shard_map/ppermute | solution.py:331
  3.6 1.6 %collective-permute-start.4 = (bf16[2,4,4,1024]{3,2,1,0:T(4,128)(2,1)}, bf16[2,4,4,1024]{3,2,1,0:T(4,128)(2,1)S(1)}, u32[]{:S(2)}, u32[]{:S(2)}) collective-permute-start(bf16[2,4,4,1024]{3,2,1,0:T(4,128)(2,1)} %param.6), channel_id=1, source_target_pairs={{0,16},{4,20},{8,24},{12,28},{16,0},{20,4},{24,8},{28,12},{1,17},{... | collective-permute-start | bytes 196616 | tf_op jit(solution)/shard_map/ppermute | solution.py:331
  5.2 1.5 %collective-permute-start.1 = (bf16[2,4,4,1024]{3,2,1,0:T(4,128)(2,1)}, bf16[2,4,4,1024]{3,2,1,0:T(4,128)(2,1)S(1)}, u32[]{:S(2)}, u32[]{:S(2)}) collective-permute-start(bf16[2,4,4,1024]{3,2,1,0:T(4,128)(2,1)} %param.6), channel_id=1, source_target_pairs={{0,4},{4,0},{8,12},{12,8},{16,20},{20,16},{24,28},{28,24},{1,5},{5... | collective-permute-start | bytes 196616 | tf_op jit(solution)/shard_map/ppermute | solution.py:331
  6.7 0.8 collective-permute-start
  7.6 0.0 collective-permute-done.2.refs_2_
  7.6 0.0 collective-permute-start.3
  7.6 0.0 collective-permute-done.6.refs_6_
  7.6 0.5 collective-permute-start.7
  8.1 0.4 collective-permute-done.4.refs_4_
  8.5 2.1 %collective-permute-start.5 = (bf16[2,4,4,1024]{3,2,1,0:T(4,128)(2,1)S(1)}, bf16[2,4,4,1024]{3,2,1,0:T(4,128)(2,1)S(1)}, u32[]{:S(2)}, u32[]{:S(2)}) collective-permute-start(bf16[2,4,4,1024]{3,2,1,0:T(4,128)(2,1)S(1)} %collective-permute-done.4.refs_4_), channel_id=1, source_target_pairs={{0,4},{4,0},{8,12},{12,8},{16,20},{20,16},{24,28},{28,24},{1,5},{5... | collective-permute-start | bytes 196616 | tf_op jit(solution)/shard_map/ppermute | solution.py:331
  10.6 0.0 collective-permute-done.1.refs_1_
  10.6 0.0 collective-permute-done.refs_0_
  10.6 0.0 collective-permute-done.3.refs_3_
  10.6 0.0 collective-permute-done.7.refs_7_
  10.6 0.9 collective-permute-done.5.refs_5_
  11.5 4.6 %predict.1 = bf16[16,4,16,128]{3,2,1,0:T(8,128)(2,1)} custom-call(bf16[2,4,4,1024]{3,2,1,0:T(4,128)(2,1)S(1)} %collective-permute-done.refs_0_, bf16[2,4,4,1024]{3,2,1,0:T(4,128)(2,1)S(1)} %collective-permute-done.1.refs_1_, bf16[2,4,4,1024]{3,2,1,0:T(4,128)(2,1)S(1)} %collective-permute-done.2.refs_2_, ...), custom_call_target="tpu_custom_call" | custom-call | tf_op jit(solution)/shard_map/predict/pallas_call | solution.py:85
  16.2 0.0 copy-start
  16.2 0.0 copy-start.1
  16.2 7.9 %all-to-all-start = ((bf16[16,4,16,128]{3,2,1,0:T(8,128)(2,1)}), bf16[16,4,16,128]{3,2,1,0:T(8,128)(2,1)S(1)}, u32[]{:S(2)}, u32[]{:S(2)}) async-start(bf16[16,4,16,128]{3,2,1,0:T(8,128)(2,1)} %predict.1), calls=%async_computation | async-start | bytes 524288 | tf_op jit(solution)/shard_map/all_to_all | solution.py:352
  24.0 0.0 copy-done.2
  24.1 0.2 convert_reduce_fusion
  24.2 2.1 %copy.8 = bf16[16,64,8,128]{3,1,0,2:T(8,128)(2,1)S(1)} copy(bf16[16,64,8,128]{3,2,1,0:T(8,128)(2,1)} %bitcast.12) | data formatting | bytes 4194304 | tf_op jit(solution)/shard_map/reshape | solution.py:354
  26.4 5.8 %all-to-all-done.parts_ref = bf16[16,4,16,128]{3,2,1,0:T(8,128)(2,1)S(1)} async-done(((bf16[16,4,16,128]{3,2,1,0:T(8,128)(2,1)}), bf16[16,4,16,128]{3,2,1,0:T(8,128)(2,1)S(1)}, u32[]{:S(2)}, u32[]{:S(2)}) %all-to-all-start) | async-done | bytes 262176 | tf_op jit(solution)/shard_map/all_to_all | solution.py:352
  32.2 0.0 copy-done
  32.2 0.0 copy-done.1
  32.2 5.3 %fit.1 = bf16[256,64,128]{2,1,0:T(8,128)(2,1)S(1)} custom-call(s32[128]{0:T(128)S(1)} %multiply_add_fusion.target_ref, bf16[16,4,16,128]{3,2,1,0:T(8,128)(2,1)S(1)} %all-to-all-done.parts_ref, bf16[128,64,128]{2,1,0:T(8,128)(2,1)S(1)} %bitcast.10, s32[1,128]{1,0:T(1,128)S(1)} %bitcast.11, bf16[1024,96]{1,0:T(8,128)(2,1)S(1)} %copy-done), custom_call_target="tpu_custom_call" | custom-call | tf_op jit(solution)/shard_map/fit/pallas_call | solution.py:282
  37.5 58.7 %all_to_all.10.given_ref = bf16[128,2,64,128]{3,2,1,0:T(8,128)(2,1)S(1)} all-to-all(bf16[128,2,64,128]{3,2,1,0:T(8,128)(2,1)S(1)} %bitcast.9), channel_id=1, replica_groups=mesh['freq'=4,'row'=8,'col'=4] {'freq','row','col'}, dimensions={0} | all-to-all | bytes 8388608 | tf_op jit(solution)/shard_map/all_to_all | solution.py:365
  96.1 2.1 %drain.1 = bf16[128,2,64,128]{3,2,1,0:T(8,128)(2,1)} custom-call(bf16[128,2,64,128]{3,2,1,0:T(8,128)(2,1)S(1)} %all_to_all.10.given_ref), custom_call_target="tpu_custom_call" | custom-call | tf_op jit(solution)/shard_map/drain/pallas_call | solution.py:318
  (1 shorter events, 0.0 us)
Async XLA Ops:
  0.0 24.0 %copy-start.2 = (s32[1,1,128,1]{2,3,1,0:T(1,128)S(1)}, s32[1,1,128,1]{2,3,1,0:T(1,128)}, u32[]{:S(2)}) copy-start(s32[1,1,128,1]{2,3,1,0:T(1,128)} %param.9) | copy-start | bytes 1540
  0.0 7.6 %collective-permute-start.2 = (bf16[2,4,4,1024]{3,2,1,0:T(4,128)(2,1)}, bf16[2,4,4,1024]{3,2,1,0:T(4,128)(2,1)S(1)}, u32[]{:S(2)}, u32[]{:S(2)}) collective-permute-start(bf16[2,4,4,1024]{3,2,1,0:T(4,128)(2,1)} %param.6), channel_id=1, source_target_pairs={{0,8},{4,12},{8,16},{12,20},{16,24},{20,28},{24,0},{28,4},{1,9},{5... | collective-permute-start | bytes 196616 | tf_op jit(solution)/shard_map/ppermute | solution.py:331
  2.1 5.5 %collective-permute-start.6 = (bf16[2,4,4,1024]{3,2,1,0:T(4,128)(2,1)}, bf16[2,4,4,1024]{3,2,1,0:T(4,128)(2,1)S(1)}, u32[]{:S(2)}, u32[]{:S(2)}) collective-permute-start(bf16[2,4,4,1024]{3,2,1,0:T(4,128)(2,1)} %param.6), channel_id=1, source_target_pairs={{0,24},{4,28},{8,0},{12,4},{16,8},{20,12},{24,16},{28,20},{1,25},{... | collective-permute-start | bytes 196616 | tf_op jit(solution)/shard_map/ppermute | solution.py:331
  3.6 4.8 %collective-permute-start.4 = (bf16[2,4,4,1024]{3,2,1,0:T(4,128)(2,1)}, bf16[2,4,4,1024]{3,2,1,0:T(4,128)(2,1)S(1)}, u32[]{:S(2)}, u32[]{:S(2)}) collective-permute-start(bf16[2,4,4,1024]{3,2,1,0:T(4,128)(2,1)} %param.6), channel_id=1, source_target_pairs={{0,16},{4,20},{8,24},{12,28},{16,0},{20,4},{24,8},{28,12},{1,17},{... | collective-permute-start | bytes 196616 | tf_op jit(solution)/shard_map/ppermute | solution.py:331
  5.2 5.4 %collective-permute-start.1 = (bf16[2,4,4,1024]{3,2,1,0:T(4,128)(2,1)}, bf16[2,4,4,1024]{3,2,1,0:T(4,128)(2,1)S(1)}, u32[]{:S(2)}, u32[]{:S(2)}) collective-permute-start(bf16[2,4,4,1024]{3,2,1,0:T(4,128)(2,1)} %param.6), channel_id=1, source_target_pairs={{0,4},{4,0},{8,12},{12,8},{16,20},{20,16},{24,28},{28,24},{1,5},{5... | collective-permute-start | bytes 196616 | tf_op jit(solution)/shard_map/ppermute | solution.py:331
  6.7 3.9 %collective-permute-start = (bf16[2,4,4,1024]{3,2,1,0:T(4,128)(2,1)}, bf16[2,4,4,1024]{3,2,1,0:T(4,128)(2,1)S(1)}, u32[]{:S(2)}, u32[]{:S(2)}) collective-permute-start(bf16[2,4,4,1024]{3,2,1,0:T(4,128)(2,1)} %param.6), channel_id=1, source_target_pairs={{0,0},{4,4},{8,8},{12,12},{16,16},{20,20},{24,24},{28,28},{1,1},{5... | collective-permute-start | bytes 196616 | tf_op jit(solution)/shard_map/ppermute | solution.py:331
  7.6 3.0 %collective-permute-start.3 = (bf16[2,4,4,1024]{3,2,1,0:T(4,128)(2,1)S(1)}, bf16[2,4,4,1024]{3,2,1,0:T(4,128)(2,1)S(1)}, u32[]{:S(2)}, u32[]{:S(2)}) collective-permute-start(bf16[2,4,4,1024]{3,2,1,0:T(4,128)(2,1)S(1)} %collective-permute-done.2.refs_2_), channel_id=1, source_target_pairs={{0,4},{4,0},{8,12},{12,8},{16,20},{20,16},{24,28},{28,24},{1,5},{5... | collective-permute-start | bytes 196616 | tf_op jit(solution)/shard_map/ppermute | solution.py:331
  7.6 3.0 %collective-permute-start.7 = (bf16[2,4,4,1024]{3,2,1,0:T(4,128)(2,1)S(1)}, bf16[2,4,4,1024]{3,2,1,0:T(4,128)(2,1)S(1)}, u32[]{:S(2)}, u32[]{:S(2)}) collective-permute-start(bf16[2,4,4,1024]{3,2,1,0:T(4,128)(2,1)S(1)} %collective-permute-done.6.refs_6_), channel_id=1, source_target_pairs={{0,4},{4,0},{8,12},{12,8},{16,20},{20,16},{24,28},{28,24},{1,5},{5... | collective-permute-start | bytes 196616 | tf_op jit(solution)/shard_map/ppermute | solution.py:331
  8.5 3.1 %collective-permute-start.5 = (bf16[2,4,4,1024]{3,2,1,0:T(4,128)(2,1)S(1)}, bf16[2,4,4,1024]{3,2,1,0:T(4,128)(2,1)S(1)}, u32[]{:S(2)}, u32[]{:S(2)}) collective-permute-start(bf16[2,4,4,1024]{3,2,1,0:T(4,128)(2,1)S(1)} %collective-permute-done.4.refs_4_), channel_id=1, source_target_pairs={{0,4},{4,0},{8,12},{12,8},{16,20},{20,16},{24,28},{28,24},{1,5},{5... | collective-permute-start | bytes 196616 | tf_op jit(solution)/shard_map/ppermute | solution.py:331
  16.2 16.0 %copy-start = (bf16[1024,96]{1,0:T(8,128)(2,1)S(1)}, bf16[1024,96]{1,0:T(8,128)(2,1)}, u32[]{:S(2)}) copy-start(bf16[1024,96]{1,0:T(8,128)(2,1)} %constant.6.clone.table_ref) | copy-start | bytes 589828
  16.2 16.0 %copy-start.1 = (s32[1,1,128]{2,1,0:T(1,128)S(1)}, s32[1,1,128]{2,1,0:T(1,128)}, u32[]{:S(2)}) copy-start(s32[1,1,128]{2,1,0:T(1,128)} %param.10) | copy-start | bytes 1540
  16.2 16.0 %all-to-all-start = ((bf16[16,4,16,128]{3,2,1,0:T(8,128)(2,1)}), bf16[16,4,16,128]{3,2,1,0:T(8,128)(2,1)S(1)}, u32[]{:S(2)}, u32[]{:S(2)}) async-start(bf16[16,4,16,128]{3,2,1,0:T(8,128)(2,1)} %predict.1), calls=%async_computation | async-start | bytes 524288 | tf_op jit(solution)/shard_map/all_to_all | solution.py:352

commit v5 on v3

--- a/solution.py
+++ b/solution.py
@@ -17,8 +17,8 @@
 WINDOWS = 128
 KEPT = 24
 DRAINS = 8
-UNROLL = 64
-AHEAD = 64
+UNROLL = 128
+AHEAD = 128
 
 
 def table_parts(bands, samples):
@@ -34,9 +34,11 @@
 
 
 def predict_kernel(*refs):
-    pieces, data_ref, out_ref = refs[:8], refs[8], refs[9]
+    pieces, data_ref, _, out_ref, ready, left = refs[:8], *refs[8:]
     first = lax.axis_index("row") // 2
-    for band in range(data_ref.shape[1]):
+    bands = data_ref.shape[1]
+    leaving = []
+    for band in range(bands):
         plain, crossed = [], []
         for piece in pieces:
             real = piece[0, band].astype(jnp.float32)
@@ -50,22 +52,48 @@
         for step in range(4):
             group = lax.rem(first + 4 - step, 4)
             for panel in range(4):
-                out_ref[group * 4 + panel, band] = total[
+                ready[band, group * 4 + panel] = total[
                     step * 16 : step * 16 + 16, panel * WIN : panel * WIN + WIN
                 ].astype(jnp.bfloat16)
-
-
-def predict(pieces, data):
+        copy = pltpu.make_async_copy(ready.at[band], out_ref.at[:, band], left.at[band])
+        copy.start()
+        leaving.append(copy)
+    for copy in leaving:
+        copy.wait()
+
+
+def marker_kernel(out_ref):
+    out_ref[...] = jnp.zeros(out_ref.shape, out_ref.dtype)
+
+
+def marker():
+    return pl.pallas_call(
+        marker_kernel,
+        out_specs=pl.BlockSpec(memory_space=pltpu.VMEM),
+        out_shape=jax.ShapeDtypeStruct((8, WIN), jnp.float32),
+        cost_estimate=pl.CostEstimate(
+            flops=10**10, bytes_accessed=64 * 1024 * 1024, transcendentals=0
+        ),
+        compiler_params=pltpu.CompilerParams(vmem_limit_bytes=1024 * 1024),
+        name="marker",
+    )()
+
+
+def predict(pieces, data, mark):
     bands = data.shape[1]
     whole = pl.BlockSpec(memory_space=pltpu.VMEM)
     return pl.pallas_call(
         predict_kernel,
-        in_specs=[whole] * 9,
-        out_specs=whole,
+        in_specs=[whole] * 10,
+        out_specs=pl.BlockSpec(memory_space=pltpu.HBM),
         out_shape=jax.ShapeDtypeStruct((16, bands, 16, WIN), jnp.bfloat16),
+        scratch_shapes=[
+            pltpu.VMEM((bands, 16, 16, WIN), jnp.bfloat16),
+            pltpu.SemaphoreType.DMA((bands,)),
+        ],
         compiler_params=pltpu.CompilerParams(vmem_limit_bytes=24 * 1024 * 1024),
         name="predict",
-    )(*pieces, data)
+    )(*pieces, data, mark)
 
 
 def fit_kernel(
@@ -304,7 +332,6 @@
     peers = lax.axis_size("row")
     own = [mine] + [moved(mine, lambda at, by=by: (at + by) % peers) for by in (2, 4, 6)]
     other = [moved(piece, lambda at: at ^ 1) for piece in own]
-    own[0] = moved(mine, lambda at: at)
     return [piece for pair in zip(own, other) for piece in pair]
 
 
@@ -317,8 +344,8 @@
 
 def local(source_rows, data_matrix, observed, window_owner, filter_len):
     devices = lax.axis_size("freq") * lax.axis_size("row") * lax.axis_size("col")
-    data = moved(data_matrix, lambda at: at)
-    partial = predict(rows_of_panel(source_rows), data)
+    mark = marker()
+    partial = predict(rows_of_panel(source_rows), data_matrix, mark)
     parts = lax.all_to_all(partial, ("freq", "col"), 0, 0, tiled=True)
     recorded = (
         observed.reshape(NT // WT, WT, ROWS_HERE, WIN).transpose(2, 0, 1, 3).reshape(-1, WT, WIN)

time: 101 us -> 99.4 us (0.984)
  starting transfers between devices: 21.6 us -> 17.8 us
  local copies, waits for them, and re-layouts: 2.15 us -> 4.29 us
  blocking collectives: 59 us -> 60.1 us
    ppermute x9 -> x7, starting transfers between devices: 13.8 us -> 10 us  [moved(): return lax.ppermute(value, 'row', pairs)]
    unnamed x6 -> x10, local copies, waits for them, and re-layouts: 0.01 us -> 2.15 us
    all_to_all x1, blocking collectives: 59 us -> 60.1 us  [local(): lax.all_to_all(buffer.reshape(devices, 2, WT, WIN), ('freq', 'row', 'col'...]
    pallas_call x1 -> x2, Pallas kernels: 2.26 us -> 2.22 us  [the longest x1 2.22 us: predict(): pl.pallas_call(predict_kernel, in_specs=[whole] * 10, out_specs=pl.BlockS...]
  transfers between devices with their start and end apart: 10 -> 8, of which waited for: 3 -> 4; matrix products, arithmetic and copies ran while one was open for 2% -> 2% of each run, Pallas kernels for 0% -> 0%
where the time goes in v5:
time: 99.4 us; the launch traced here: 99.1 us
  blocking collectives  60.1 us (60%)
  starting transfers between devices  17.8 us (18%)
  Pallas kernels  9.53 us (10%)
  waiting for transfers between devices  7.2 us (7%)
  local copies, waits for them, and re-layouts  4.29 us (4%)
    all_to_all x1, blocking collectives, local(): lax.all_to_all(buffer.reshape(devices, 2, WT, WIN), ('freq', 'row', 'col'...  60.1 us
    ppermute x7, starting transfers between devices, moved(): return lax.ppermute(value, 'row', pairs)  10 us
    all_to_all x1, starting transfers between devices, local(): parts = lax.all_to_all(partial, ('freq', 'col'), 0, 0, tiled=True)  7.74 us
    all_to_all x1, waiting for transfers between devices, local(): parts = lax.all_to_all(partial, ('freq', 'col'), 0, 0, tiled=True)  5.65 us
    pallas_call x1, Pallas kernels, fit(): pl.pallas_call(fit_kernel, in_specs=[pl.BlockSpec(memory_space=pltpu.SMEM...  5.24 us
    pallas_call x1, Pallas kernels, predict(): pl.pallas_call(predict_kernel, in_specs=[whole] * 10, out_specs=pl.BlockS...  2.22 us
    unnamed x10, local copies, waits for them, and re-layouts  2.15 us
    reshape x1, local copies, waits for them, and re-layouts, local(): observed.reshape(NT // WT, WT, ROWS_HERE, WIN).transpose(2, 0, 1, 3)  2.14 us
  transfers between devices with their start and end apart: 8, of which 4 were waited for; matrix products, arithmetic and copies ran while one was open for 2% of the time, Pallas kernels for 0%

profile of v5, /device:TPU:1, one launch (start us, length us, event | category | flops | bytes accessed | tf_op | source)
XLA Modules:
  0.0 99.1 jit_solution(7796835225537075676)
XLA Ops:
  0.0 0.0 copy-start.2
  0.0 3.7 %collective-permute-start.3 = (bf16[2,4,4,1024]{3,2,1,0:T(4,128)(2,1)}, bf16[2,4,4,1024]{3,2,1,0:T(4,128)(2,1)S(1)}, u32[]{:S(2)}, u32[]{:S(2)}) collective-permute-start(bf16[2,4,4,1024]{3,2,1,0:T(4,128)(2,1)} %refs_0_.1), channel_id=1, source_target_pairs={{0,16},{4,20},{8,24},{12,28},{16,0},{20,4},{24,8},{28,12},{1,17},{... | collective-permute-start | bytes 196616 | tf_op jit(solution)/shard_map/ppermute | solution.py:328
  3.7 0.4 collective-permute-start.1
  4.1 2.3 %collective-permute-start.5 = (bf16[2,4,4,1024]{3,2,1,0:T(4,128)(2,1)}, bf16[2,4,4,1024]{3,2,1,0:T(4,128)(2,1)S(1)}, u32[]{:S(2)}, u32[]{:S(2)}) collective-permute-start(bf16[2,4,4,1024]{3,2,1,0:T(4,128)(2,1)} %refs_0_.1), channel_id=1, source_target_pairs={{0,24},{4,28},{8,0},{12,4},{16,8},{20,12},{24,16},{28,20},{1,25},{... | collective-permute-start | bytes 196616 | tf_op jit(solution)/shard_map/ppermute | solution.py:328
  6.4 1.5 %collective-permute-start = (bf16[2,4,4,1024]{3,2,1,0:T(4,128)(2,1)}, bf16[2,4,4,1024]{3,2,1,0:T(4,128)(2,1)S(1)}, u32[]{:S(2)}, u32[]{:S(2)}) collective-permute-start(bf16[2,4,4,1024]{3,2,1,0:T(4,128)(2,1)} %refs_0_.1), channel_id=1, source_target_pairs={{0,4},{4,0},{8,12},{12,8},{16,20},{20,16},{24,28},{28,24},{1,5},{5... | collective-permute-start | bytes 196616 | tf_op jit(solution)/shard_map/ppermute | solution.py:328
  7.9 0.0 collective-permute-done.3.refs_4_
  7.9 0.0 collective-permute-start.4
  7.9 0.3 collective-permute-done.1.refs_2_
  8.3 2.1 %collective-permute-start.2 = (bf16[2,4,4,1024]{3,2,1,0:T(4,128)(2,1)S(1)}, bf16[2,4,4,1024]{3,2,1,0:T(4,128)(2,1)S(1)}, u32[]{:S(2)}, u32[]{:S(2)}) collective-permute-start(bf16[2,4,4,1024]{3,2,1,0:T(4,128)(2,1)S(1)} %collective-permute-done.1.refs_2_), channel_id=1, source_target_pairs={{0,4},{4,0},{8,12},{12,8},{16,20},{20,16},{24,28},{28,24},{1,5},{5... | collective-permute-start | bytes 196616 | tf_op jit(solution)/shard_map/ppermute | solution.py:328
  10.4 0.0 collective-permute-done.5.refs_6_
  10.4 0.0 collective-permute-start.6
  10.4 0.0 copy-start
  10.4 0.0 copy-start.4
  10.4 0.0 collective-permute-done.refs_1_
  10.4 0.0 collective-permute-done.4.refs_5_
  10.4 0.8 collective-permute-done.2.refs_3_
  11.3 0.4 collective-permute-done.6.refs_7_
  11.6 0.0 copy-done.2
  11.6 2.1 %copy-done = bf16[2,4,1024,512]{3,2,1,0:T(8,128)(2,1)S(1)} copy-done((bf16[2,4,1024,512]{3,2,1,0:T(8,128)(2,1)S(1)}, bf16[2,4,1024,512]{3,2,1,0:T(8,128)(2,1)}, u32[]{:S(2)}) %copy-start) | copy-done | bytes 8388632
  13.8 2.2 %predict.1 = bf16[16,4,16,128]{3,2,1,0:T(8,128)(2,1)} custom-call(bf16[2,4,4,1024]{3,2,1,0:T(4,128)(2,1)S(1)} %copy-done.2, bf16[2,4,4,1024]{3,2,1,0:T(4,128)(2,1)S(1)} %collective-permute-done.refs_1_, bf16[2,4,4,1024]{3,2,1,0:T(4,128)(2,1)S(1)} %collective-permute-done.1.refs_2_, bf16[2,4,4,1024]{3,2,1,0:T(4,128)(2,1)S(1)} %collective-permute-done.2.refs_3_, ...), custom_call_target="tpu_custom_call" | custom-call | tf_op jit(solution)/shard_map/predict/pallas_call | solution.py:85
  16.0 0.0 copy-start.1
  16.0 0.0 copy-start.3
  16.0 7.7 %all-to-all-start = ((bf16[16,4,16,128]{3,2,1,0:T(8,128)(2,1)}), bf16[16,4,16,128]{3,2,1,0:T(8,128)(2,1)S(1)}, u32[]{:S(2)}, u32[]{:S(2)}) async-start(bf16[16,4,16,128]{3,2,1,0:T(8,128)(2,1)} %predict.1), calls=%async_computation | async-start | bytes 524288 | tf_op jit(solution)/shard_map/all_to_all | solution.py:349
  23.8 0.0 copy-done.4
  23.8 0.2 convert_reduce_fusion
  24.0 2.1 %copy.8 = bf16[16,64,8,128]{3,1,0,2:T(8,128)(2,1)S(1)} copy(bf16[16,64,8,128]{3,2,1,0:T(8,128)(2,1)} %bitcast.12) | data formatting | bytes 4194304 | tf_op jit(solution)/shard_map/reshape | solution.py:351
  26.1 5.6 %all-to-all-done.parts_ref = bf16[16,4,16,128]{3,2,1,0:T(8,128)(2,1)S(1)} async-done(((bf16[16,4,16,128]{3,2,1,0:T(8,128)(2,1)}), bf16[16,4,16,128]{3,2,1,0:T(8,128)(2,1)S(1)}, u32[]{:S(2)}, u32[]{:S(2)}) %all-to-all-start) | async-done | bytes 262176 | tf_op jit(solution)/shard_map/all_to_all | solution.py:349
  31.8 0.0 copy-done.1
  31.8 0.0 copy-done.3
  31.8 5.2 %fit.1 = bf16[256,64,128]{2,1,0:T(8,128)(2,1)S(1)} custom-call(s32[128]{0:T(128)S(1)} %multiply_add_fusion.target_ref, bf16[16,4,16,128]{3,2,1,0:T(8,128)(2,1)S(1)} %all-to-all-done.parts_ref, bf16[128,64,128]{2,1,0:T(8,128)(2,1)S(1)} %bitcast.10, s32[1,128]{1,0:T(1,128)S(1)} %bitcast.11, bf16[1024,96]{1,0:T(8,128)(2,1)S(1)} %copy-done.1), custom_call_target="tpu_custom_call" | custom-call | tf_op jit(solution)/shard_map/fit/pallas_call | solution.py:279
  37.0 60.1 %all_to_all.10.given_ref = bf16[128,2,64,128]{3,2,1,0:T(8,128)(2,1)S(1)} all-to-all(bf16[128,2,64,128]{3,2,1,0:T(8,128)(2,1)S(1)} %bitcast.9), channel_id=1, replica_groups=mesh['freq'=4,'row'=8,'col'=4] {'freq','row','col'}, dimensions={0} | all-to-all | bytes 8388608 | tf_op jit(solution)/shard_map/all_to_all | solution.py:362
  97.1 2.1 %drain.1 = bf16[128,2,64,128]{3,2,1,0:T(8,128)(2,1)} custom-call(bf16[128,2,64,128]{3,2,1,0:T(8,128)(2,1)S(1)} %all_to_all.10.given_ref), custom_call_target="tpu_custom_call" | custom-call | tf_op jit(solution)/shard_map/drain/pallas_call | solution.py:315
  (2 shorter events, 0.0 us)
Async XLA Ops:
  0.0 11.6 %copy-start.2 = (bf16[2,4,4,1024]{3,2,1,0:T(4,128)(2,1)S(1)}, bf16[2,4,4,1024]{3,2,1,0:T(4,128)(2,1)}, u32[]{:S(2)}) copy-start(bf16[2,4,4,1024]{3,2,1,0:T(4,128)(2,1)} %refs_0_.1) | copy-start | bytes 196612
  0.0 7.9 %collective-permute-start.3 = (bf16[2,4,4,1024]{3,2,1,0:T(4,128)(2,1)}, bf16[2,4,4,1024]{3,2,1,0:T(4,128)(2,1)S(1)}, u32[]{:S(2)}, u32[]{:S(2)}) collective-permute-start(bf16[2,4,4,1024]{3,2,1,0:T(4,128)(2,1)} %refs_0_.1), channel_id=1, source_target_pairs={{0,16},{4,20},{8,24},{12,28},{16,0},{20,4},{24,8},{28,12},{1,17},{... | collective-permute-start | bytes 196616 | tf_op jit(solution)/shard_map/ppermute | solution.py:328
  3.7 4.5 %collective-permute-start.1 = (bf16[2,4,4,1024]{3,2,1,0:T(4,128)(2,1)}, bf16[2,4,4,1024]{3,2,1,0:T(4,128)(2,1)S(1)}, u32[]{:S(2)}, u32[]{:S(2)}) collective-permute-start(bf16[2,4,4,1024]{3,2,1,0:T(4,128)(2,1)} %refs_0_.1), channel_id=1, source_target_pairs={{0,8},{4,12},{8,16},{12,20},{16,24},{20,28},{24,0},{28,4},{1,9},{5... | collective-permute-start | bytes 196616 | tf_op jit(solution)/shard_map/ppermute | solution.py:328
  4.1 6.2 %collective-permute-start.5 = (bf16[2,4,4,1024]{3,2,1,0:T(4,128)(2,1)}, bf16[2,4,4,1024]{3,2,1,0:T(4,128)(2,1)S(1)}, u32[]{:S(2)}, u32[]{:S(2)}) collective-permute-start(bf16[2,4,4,1024]{3,2,1,0:T(4,128)(2,1)} %refs_0_.1), channel_id=1, source_target_pairs={{0,24},{4,28},{8,0},{12,4},{16,8},{20,12},{24,16},{28,20},{1,25},{... | collective-permute-start | bytes 196616 | tf_op jit(solution)/shard_map/ppermute | solution.py:328
  6.4 4.0 %collective-permute-start = (bf16[2,4,4,1024]{3,2,1,0:T(4,128)(2,1)}, bf16[2,4,4,1024]{3,2,1,0:T(4,128)(2,1)S(1)}, u32[]{:S(2)}, u32[]{:S(2)}) collective-permute-start(bf16[2,4,4,1024]{3,2,1,0:T(4,128)(2,1)} %refs_0_.1), channel_id=1, source_target_pairs={{0,4},{4,0},{8,12},{12,8},{16,20},{20,16},{24,28},{28,24},{1,5},{5... | collective-permute-start | bytes 196616 | tf_op jit(solution)/shard_map/ppermute | solution.py:328
  7.9 2.5 %collective-permute-start.4 = (bf16[2,4,4,1024]{3,2,1,0:T(4,128)(2,1)S(1)}, bf16[2,4,4,1024]{3,2,1,0:T(4,128)(2,1)S(1)}, u32[]{:S(2)}, u32[]{:S(2)}) collective-permute-start(bf16[2,4,4,1024]{3,2,1,0:T(4,128)(2,1)S(1)} %collective-permute-done.3.refs_4_), channel_id=1, source_target_pairs={{0,4},{4,0},{8,12},{12,8},{16,20},{20,16},{24,28},{28,24},{1,5},{5... | collective-permute-start | bytes 196616 | tf_op jit(solution)/shard_map/ppermute | solution.py:328
  8.3 3.0 %collective-permute-start.2 = (bf16[2,4,4,1024]{3,2,1,0:T(4,128)(2,1)S(1)}, bf16[2,4,4,1024]{3,2,1,0:T(4,128)(2,1)S(1)}, u32[]{:S(2)}, u32[]{:S(2)}) collective-permute-start(bf16[2,4,4,1024]{3,2,1,0:T(4,128)(2,1)S(1)} %collective-permute-done.1.refs_2_), channel_id=1, source_target_pairs={{0,4},{4,0},{8,12},{12,8},{16,20},{20,16},{24,28},{28,24},{1,5},{5... | collective-permute-start | bytes 196616 | tf_op jit(solution)/shard_map/ppermute | solution.py:328
  10.4 1.3 %collective-permute-start.6 = (bf16[2,4,4,1024]{3,2,1,0:T(4,128)(2,1)S(1)}, bf16[2,4,4,1024]{3,2,1,0:T(4,128)(2,1)S(1)}, u32[]{:S(2)}, u32[]{:S(2)}) collective-permute-start(bf16[2,4,4,1024]{3,2,1,0:T(4,128)(2,1)S(1)} %collective-permute-done.5.refs_6_), channel_id=1, source_target_pairs={{0,4},{4,0},{8,12},{12,8},{16,20},{20,16},{24,28},{28,24},{1,5},{5... | collective-permute-start | bytes 196616 | tf_op jit(solution)/shard_map/ppermute | solution.py:328
  10.4 3.4 %copy-start = (bf16[2,4,1024,512]{3,2,1,0:T(8,128)(2,1)S(1)}, bf16[2,4,1024,512]{3,2,1,0:T(8,128)(2,1)}, u32[]{:S(2)}) copy-start(bf16[2,4,1024,512]{3,2,1,0:T(8,128)(2,1)} %refs_8_.1) | copy-start | bytes 25165828
  10.4 13.4 %copy-start.4 = (s32[1,1,128,1]{2,3,1,0:T(1,128)S(1)}, s32[1,1,128,1]{2,3,1,0:T(1,128)}, u32[]{:S(2)}) copy-start(s32[1,1,128,1]{2,3,1,0:T(1,128)} %param.9) | copy-start | bytes 1540
  16.0 15.8 %copy-start.1 = (bf16[1024,96]{1,0:T(8,128)(2,1)S(1)}, bf16[1024,96]{1,0:T(8,128)(2,1)}, u32[]{:S(2)}) copy-start(bf16[1024,96]{1,0:T(8,128)(2,1)} %constant.6.clone.table_ref) | copy-start | bytes 589828
  16.0 15.8 %copy-start.3 = (s32[1,1,128]{2,1,0:T(1,128)S(1)}, s32[1,1,128]{2,1,0:T(1,128)}, u32[]{:S(2)}) copy-start(s32[1,1,128]{2,1,0:T(1,128)} %param.10) | copy-start | bytes 1540
  16.0 15.7 %all-to-all-start = ((bf16[16,4,16,128]{3,2,1,0:T(8,128)(2,1)}), bf16[16,4,16,128]{3,2,1,0:T(8,128)(2,1)S(1)}, u32[]{:S(2)}, u32[]{:S(2)}) async-start(bf16[16,4,16,128]{3,2,1,0:T(8,128)(2,1)} %predict.1), calls=%async_computation | async-start | bytes 524288 | tf_op jit(solution)/shard_map/all_to_all | solution.py:349

commit v6 on v5

--- a/solution.py
+++ b/solution.py
@@ -17,8 +17,6 @@
 WINDOWS = 128
 KEPT = 24
 DRAINS = 8
-UNROLL = 128
-AHEAD = 128
 
 
 def table_parts(bands, samples):
@@ -138,7 +136,7 @@
 
     mirror = 7 - lax.broadcasted_iota(jnp.int32, (8, WIN), 0)
 
-    def traces_of(pair, _):
+    def traces_of(pair):
         traces = jnp.dot(
             table_ref[...], stacked[pair], preferred_element_type=jnp.float32
         )
@@ -159,21 +157,18 @@
         for at in range(2):
             field[2 * pair + at, :NT] = traces[:, at * WIN : at * WIN + WIN].astype(jnp.bfloat16)
             field[2 * pair + at, NT:] = turned[:, at * WIN : at * WIN + WIN].astype(jnp.bfloat16)
-        return 0
-
-    lax.fori_loop(0, ROWS_HERE // 2, traces_of, 0)
 
     def window_at(index):
         row, part = index // (NT // WT), index % (NT // WT)
-        return row, pl.multiple_of(part * WT, WT)
+        return row, part * WT
 
     none = jnp.zeros((WT, WIN), jnp.bfloat16)
     share = out_ref.shape[0] // WINDOWS
 
-    def correlate(step, _):
-        for inner in range(0, AHEAD, 2):
+    def correlate(pair):
+        for inner in range(pair * 32, pair * 32 + 32, 2):
             aheads, backs, records = [], [], []
-            for index in (step * AHEAD + inner, step * AHEAD + inner + 1):
+            for index in (inner, inner + 1):
                 row, start = window_at(index)
                 aheads.append(field[row, pl.ds(start, WT), :])
                 backs.append(field[row, pl.ds(start + NT, WT), :])
@@ -193,20 +188,27 @@
                 preferred_element_type=jnp.float32,
             )
             for at in range(2):
-                index = step * AHEAD + inner + at
+                index = inner + at
                 turned = pltpu.roll(
                     products[at * WT : at * WT + WT], 1, 1, stride=1, stride_axis=0
                 )
-                out_ref[pl.ds(index * share, share)] = jnp.zeros((share, WT, WIN), jnp.bfloat16)
+                zero = jnp.minimum(jnp.maximum(turned[:16], 0.0), 0.0).astype(jnp.bfloat16)
+                zero = jnp.concatenate([zero] * (WT // 16), axis=0)
+                for slot in range(share):
+                    out_ref[index * share + slot] = zero
                 rest = turned[16:24]
                 for block in range(3, 8):
                     rest += turned[block * 8 : block * 8 + 8]
-                kept[pl.ds(pl.multiple_of(index * KEPT, 8), KEPT), :] = jnp.concatenate(
+                kept[pl.ds(index * KEPT, KEPT), :] = jnp.concatenate(
                     [turned[:16], rest], axis=0
                 )
-        return 0
-
-    lax.fori_loop(0, WINDOWS // AHEAD, correlate, 0)
+
+    for pair in range(ROWS_HERE // 2):
+        if pair == 0:
+            traces_of(0)
+        if pair + 1 < ROWS_HERE // 2:
+            traces_of(pair + 1)
+        correlate(pair)
 
     rest = kept[pl.ds(16, WINDOWS, stride=KEPT), :]
     for block in range(1, 8):
@@ -254,9 +256,8 @@
     samples = lax.broadcasted_iota(jnp.int32, (16, WIN), 0)
     inside = (lanes % WT) <= samples
 
-    def subtract(step, _):
-        for inner in range(UNROLL):
-            index = step * UNROLL + inner
+    def subtract():
+        for index in range(WINDOWS):
             row, start = window_at(index)
             ahead = field[row, pl.ds(start, WT), :]
             line = jnp.broadcast_to(filters[pl.ds(index, 1), :], (WT, WIN))
@@ -269,9 +270,8 @@
             )
             left = recorded_ref[index].astype(jnp.float32) - ahead.astype(jnp.float32)
             out_ref[target_ref[index]] = (left - shaped).astype(jnp.bfloat16)
-        return 0
-
-    lax.fori_loop(0, WINDOWS // UNROLL, subtract, 0)
+
+    subtract()
 
 
 def fit(target, parts, recorded, lengths, table, slots):

time: 99.4 us -> 98.4 us (0.990)
  no operation moved by 1% of the time
where the time goes in v6:
time: 98.4 us; the launch traced here: 98.2 us
  blocking collectives  60.1 us (61%)
  starting transfers between devices  17.8 us (18%)
  Pallas kernels  8.59 us (9%)
  waiting for transfers between devices  7.2 us (7%)
  local copies, waits for them, and re-layouts  4.29 us (4%)
    all_to_all x1, blocking collectives, local(): lax.all_to_all(buffer.reshape(devices, 2, WT, WIN), ('freq', 'row', 'col'...  60.1 us
    ppermute x7, starting transfers between devices, moved(): return lax.ppermute(value, 'row', pairs)  10 us
    all_to_all x1, starting transfers between devices, local(): parts = lax.all_to_all(partial, ('freq', 'col'), 0, 0, tiled=True)  7.74 us
    all_to_all x1, waiting for transfers between devices, local(): parts = lax.all_to_all(partial, ('freq', 'col'), 0, 0, tiled=True)  5.65 us
    pallas_call x1, Pallas kernels, fit(): pl.pallas_call(fit_kernel, in_specs=[pl.BlockSpec(memory_space=pltpu.SMEM...  4.3 us
    pallas_call x1, Pallas kernels, predict(): pl.pallas_call(predict_kernel, in_specs=[whole] * 10, out_specs=pl.BlockS...  2.22 us
    unnamed x10, local copies, waits for them, and re-layouts  2.15 us
    reshape x1, local copies, waits for them, and re-layouts, local(): observed.reshape(NT // WT, WT, ROWS_HERE, WIN).transpose(2, 0, 1, 3)  2.14 us
  transfers between devices with their start and end apart: 8, of which 4 were waited for; matrix products, arithmetic and copies ran while one was open for 2% of the time, Pallas kernels for 0%

profile of v6, /device:TPU:1, one launch (start us, length us, event | category | flops | bytes accessed | tf_op | source)
XLA Modules:
  0.0 98.2 jit_solution(2989597390402761418)
XLA Ops:
  0.0 0.0 copy-start.2
  0.0 3.7 %collective-permute-start.3 = (bf16[2,4,4,1024]{3,2,1,0:T(4,128)(2,1)}, bf16[2,4,4,1024]{3,2,1,0:T(4,128)(2,1)S(1)}, u32[]{:S(2)}, u32[]{:S(2)}) collective-permute-start(bf16[2,4,4,1024]{3,2,1,0:T(4,128)(2,1)} %refs_0_.1), channel_id=1, source_target_pairs={{0,16},{4,20},{8,24},{12,28},{16,0},{20,4},{24,8},{28,12},{1,17},{... | collective-permute-start | bytes 196616 | tf_op jit(solution)/shard_map/ppermute | solution.py:328
  3.7 0.4 collective-permute-start.1
  4.1 2.3 %collective-permute-start.5 = (bf16[2,4,4,1024]{3,2,1,0:T(4,128)(2,1)}, bf16[2,4,4,1024]{3,2,1,0:T(4,128)(2,1)S(1)}, u32[]{:S(2)}, u32[]{:S(2)}) collective-permute-start(bf16[2,4,4,1024]{3,2,1,0:T(4,128)(2,1)} %refs_0_.1), channel_id=1, source_target_pairs={{0,24},{4,28},{8,0},{12,4},{16,8},{20,12},{24,16},{28,20},{1,25},{... | collective-permute-start | bytes 196616 | tf_op jit(solution)/shard_map/ppermute | solution.py:328
  6.4 1.5 %collective-permute-start = (bf16[2,4,4,1024]{3,2,1,0:T(4,128)(2,1)}, bf16[2,4,4,1024]{3,2,1,0:T(4,128)(2,1)S(1)}, u32[]{:S(2)}, u32[]{:S(2)}) collective-permute-start(bf16[2,4,4,1024]{3,2,1,0:T(4,128)(2,1)} %refs_0_.1), channel_id=1, source_target_pairs={{0,4},{4,0},{8,12},{12,8},{16,20},{20,16},{24,28},{28,24},{1,5},{5... | collective-permute-start | bytes 196616 | tf_op jit(solution)/shard_map/ppermute | solution.py:328
  7.9 0.0 collective-permute-done.3.refs_4_
  7.9 0.0 collective-permute-start.4
  7.9 0.3 collective-permute-done.1.refs_2_
  8.3 2.1 %collective-permute-start.2 = (bf16[2,4,4,1024]{3,2,1,0:T(4,128)(2,1)S(1)}, bf16[2,4,4,1024]{3,2,1,0:T(4,128)(2,1)S(1)}, u32[]{:S(2)}, u32[]{:S(2)}) collective-permute-start(bf16[2,4,4,1024]{3,2,1,0:T(4,128)(2,1)S(1)} %collective-permute-done.1.refs_2_), channel_id=1, source_target_pairs={{0,4},{4,0},{8,12},{12,8},{16,20},{20,16},{24,28},{28,24},{1,5},{5... | collective-permute-start | bytes 196616 | tf_op jit(solution)/shard_map/ppermute | solution.py:328
  10.4 0.0 collective-permute-done.5.refs_6_
  10.4 0.0 collective-permute-start.6
  10.4 0.0 copy-start
  10.4 0.0 copy-start.4
  10.4 0.0 collective-permute-done.refs_1_
  10.4 0.0 collective-permute-done.4.refs_5_
  10.4 0.8 collective-permute-done.2.refs_3_
  11.3 0.4 collective-permute-done.6.refs_7_
  11.6 0.0 copy-done.2
  11.6 2.1 %copy-done = bf16[2,4,1024,512]{3,2,1,0:T(8,128)(2,1)S(1)} copy-done((bf16[2,4,1024,512]{3,2,1,0:T(8,128)(2,1)S(1)}, bf16[2,4,1024,512]{3,2,1,0:T(8,128)(2,1)}, u32[]{:S(2)}) %copy-start) | copy-done | bytes 8388632
  13.8 2.2 %predict.1 = bf16[16,4,16,128]{3,2,1,0:T(8,128)(2,1)} custom-call(bf16[2,4,4,1024]{3,2,1,0:T(4,128)(2,1)S(1)} %copy-done.2, bf16[2,4,4,1024]{3,2,1,0:T(4,128)(2,1)S(1)} %collective-permute-done.refs_1_, bf16[2,4,4,1024]{3,2,1,0:T(4,128)(2,1)S(1)} %collective-permute-done.1.refs_2_, bf16[2,4,4,1024]{3,2,1,0:T(4,128)(2,1)S(1)} %collective-permute-done.2.refs_3_, ...), custom_call_target="tpu_custom_call" | custom-call | tf_op jit(solution)/shard_map/predict/pallas_call | solution.py:83
  16.0 0.0 copy-start.1
  16.0 0.0 copy-start.3
  16.0 7.7 %all-to-all-start = ((bf16[16,4,16,128]{3,2,1,0:T(8,128)(2,1)}), bf16[16,4,16,128]{3,2,1,0:T(8,128)(2,1)S(1)}, u32[]{:S(2)}, u32[]{:S(2)}) async-start(bf16[16,4,16,128]{3,2,1,0:T(8,128)(2,1)} %predict.1), calls=%async_computation | async-start | bytes 524288 | tf_op jit(solution)/shard_map/all_to_all | solution.py:349
  23.8 0.0 copy-done.4
  23.8 0.2 convert_reduce_fusion
  24.0 2.1 %copy.8 = bf16[16,64,8,128]{3,1,0,2:T(8,128)(2,1)S(1)} copy(bf16[16,64,8,128]{3,2,1,0:T(8,128)(2,1)} %bitcast.12) | data formatting | bytes 4194304 | tf_op jit(solution)/shard_map/reshape | solution.py:351
  26.1 5.6 %all-to-all-done.parts_ref = bf16[16,4,16,128]{3,2,1,0:T(8,128)(2,1)S(1)} async-done(((bf16[16,4,16,128]{3,2,1,0:T(8,128)(2,1)}), bf16[16,4,16,128]{3,2,1,0:T(8,128)(2,1)S(1)}, u32[]{:S(2)}, u32[]{:S(2)}) %all-to-all-start) | async-done | bytes 262176 | tf_op jit(solution)/shard_map/all_to_all | solution.py:349
  31.8 0.0 copy-done.1
  31.8 0.0 copy-done.3
  31.8 4.3 %fit.1 = bf16[256,64,128]{2,1,0:T(8,128)(2,1)S(1)} custom-call(s32[128]{0:T(128)S(1)} %multiply_add_fusion.target_ref, bf16[16,4,16,128]{3,2,1,0:T(8,128)(2,1)S(1)} %all-to-all-done.parts_ref, bf16[128,64,128]{2,1,0:T(8,128)(2,1)S(1)} %bitcast.10, s32[1,128]{1,0:T(1,128)S(1)} %bitcast.11, bf16[1024,96]{1,0:T(8,128)(2,1)S(1)} %copy-done.1), custom_call_target="tpu_custom_call" | custom-call | tf_op jit(solution)/shard_map/fit/pallas_call | solution.py:279
  36.1 60.1 %all_to_all.10.given_ref = bf16[128,2,64,128]{3,2,1,0:T(8,128)(2,1)S(1)} all-to-all(bf16[128,2,64,128]{3,2,1,0:T(8,128)(2,1)S(1)} %bitcast.9), channel_id=1, replica_groups=mesh['freq'=4,'row'=8,'col'=4] {'freq','row','col'}, dimensions={0} | all-to-all | bytes 8388608 | tf_op jit(solution)/shard_map/all_to_all | solution.py:362
  96.1 2.1 %drain.1 = bf16[128,2,64,128]{3,2,1,0:T(8,128)(2,1)} custom-call(bf16[128,2,64,128]{3,2,1,0:T(8,128)(2,1)S(1)} %all_to_all.10.given_ref), custom_call_target="tpu_custom_call" | custom-call | tf_op jit(solution)/shard_map/drain/pallas_call | solution.py:315
  (2 shorter events, 0.0 us)
Async XLA Ops:
  0.0 11.6 %copy-start.2 = (bf16[2,4,4,1024]{3,2,1,0:T(4,128)(2,1)S(1)}, bf16[2,4,4,1024]{3,2,1,0:T(4,128)(2,1)}, u32[]{:S(2)}) copy-start(bf16[2,4,4,1024]{3,2,1,0:T(4,128)(2,1)} %refs_0_.1) | copy-start | bytes 196612
  0.0 7.9 %collective-permute-start.3 = (bf16[2,4,4,1024]{3,2,1,0:T(4,128)(2,1)}, bf16[2,4,4,1024]{3,2,1,0:T(4,128)(2,1)S(1)}, u32[]{:S(2)}, u32[]{:S(2)}) collective-permute-start(bf16[2,4,4,1024]{3,2,1,0:T(4,128)(2,1)} %refs_0_.1), channel_id=1, source_target_pairs={{0,16},{4,20},{8,24},{12,28},{16,0},{20,4},{24,8},{28,12},{1,17},{... | collective-permute-start | bytes 196616 | tf_op jit(solution)/shard_map/ppermute | solution.py:328
  3.7 4.5 %collective-permute-start.1 = (bf16[2,4,4,1024]{3,2,1,0:T(4,128)(2,1)}, bf16[2,4,4,1024]{3,2,1,0:T(4,128)(2,1)S(1)}, u32[]{:S(2)}, u32[]{:S(2)}) collective-permute-start(bf16[2,4,4,1024]{3,2,1,0:T(4,128)(2,1)} %refs_0_.1), channel_id=1, source_target_pairs={{0,8},{4,12},{8,16},{12,20},{16,24},{20,28},{24,0},{28,4},{1,9},{5... | collective-permute-start | bytes 196616 | tf_op jit(solution)/shard_map/ppermute | solution.py:328
  4.1 6.2 %collective-permute-start.5 = (bf16[2,4,4,1024]{3,2,1,0:T(4,128)(2,1)}, bf16[2,4,4,1024]{3,2,1,0:T(4,128)(2,1)S(1)}, u32[]{:S(2)}, u32[]{:S(2)}) collective-permute-start(bf16[2,4,4,1024]{3,2,1,0:T(4,128)(2,1)} %refs_0_.1), channel_id=1, source_target_pairs={{0,24},{4,28},{8,0},{12,4},{16,8},{20,12},{24,16},{28,20},{1,25},{... | collective-permute-start | bytes 196616 | tf_op jit(solution)/shard_map/ppermute | solution.py:328
  6.4 4.0 %collective-permute-start = (bf16[2,4,4,1024]{3,2,1,0:T(4,128)(2,1)}, bf16[2,4,4,1024]{3,2,1,0:T(4,128)(2,1)S(1)}, u32[]{:S(2)}, u32[]{:S(2)}) collective-permute-start(bf16[2,4,4,1024]{3,2,1,0:T(4,128)(2,1)} %refs_0_.1), channel_id=1, source_target_pairs={{0,4},{4,0},{8,12},{12,8},{16,20},{20,16},{24,28},{28,24},{1,5},{5... | collective-permute-start | bytes 196616 | tf_op jit(solution)/shard_map/ppermute | solution.py:328
  7.9 2.5 %collective-permute-start.4 = (bf16[2,4,4,1024]{3,2,1,0:T(4,128)(2,1)S(1)}, bf16[2,4,4,1024]{3,2,1,0:T(4,128)(2,1)S(1)}, u32[]{:S(2)}, u32[]{:S(2)}) collective-permute-start(bf16[2,4,4,1024]{3,2,1,0:T(4,128)(2,1)S(1)} %collective-permute-done.3.refs_4_), channel_id=1, source_target_pairs={{0,4},{4,0},{8,12},{12,8},{16,20},{20,16},{24,28},{28,24},{1,5},{5... | collective-permute-start | bytes 196616 | tf_op jit(solution)/shard_map/ppermute | solution.py:328
  8.3 3.0 %collective-permute-start.2 = (bf16[2,4,4,1024]{3,2,1,0:T(4,128)(2,1)S(1)}, bf16[2,4,4,1024]{3,2,1,0:T(4,128)(2,1)S(1)}, u32[]{:S(2)}, u32[]{:S(2)}) collective-permute-start(bf16[2,4,4,1024]{3,2,1,0:T(4,128)(2,1)S(1)} %collective-permute-done.1.refs_2_), channel_id=1, source_target_pairs={{0,4},{4,0},{8,12},{12,8},{16,20},{20,16},{24,28},{28,24},{1,5},{5... | collective-permute-start | bytes 196616 | tf_op jit(solution)/shard_map/ppermute | solution.py:328
  10.4 1.3 %collective-permute-start.6 = (bf16[2,4,4,1024]{3,2,1,0:T(4,128)(2,1)S(1)}, bf16[2,4,4,1024]{3,2,1,0:T(4,128)(2,1)S(1)}, u32[]{:S(2)}, u32[]{:S(2)}) collective-permute-start(bf16[2,4,4,1024]{3,2,1,0:T(4,128)(2,1)S(1)} %collective-permute-done.5.refs_6_), channel_id=1, source_target_pairs={{0,4},{4,0},{8,12},{12,8},{16,20},{20,16},{24,28},{28,24},{1,5},{5... | collective-permute-start | bytes 196616 | tf_op jit(solution)/shard_map/ppermute | solution.py:328
  10.4 3.4 %copy-start = (bf16[2,4,1024,512]{3,2,1,0:T(8,128)(2,1)S(1)}, bf16[2,4,1024,512]{3,2,1,0:T(8,128)(2,1)}, u32[]{:S(2)}) copy-start(bf16[2,4,1024,512]{3,2,1,0:T(8,128)(2,1)} %refs_8_.1) | copy-start | bytes 25165828
  10.4 13.4 %copy-start.4 = (s32[1,1,128,1]{2,3,1,0:T(1,128)S(1)}, s32[1,1,128,1]{2,3,1,0:T(1,128)}, u32[]{:S(2)}) copy-start(s32[1,1,128,1]{2,3,1,0:T(1,128)} %param.9) | copy-start | bytes 1540
  16.0 15.8 %copy-start.1 = (bf16[1024,96]{1,0:T(8,128)(2,1)S(1)}, bf16[1024,96]{1,0:T(8,128)(2,1)}, u32[]{:S(2)}) copy-start(bf16[1024,96]{1,0:T(8,128)(2,1)} %constant.6.clone.table_ref) | copy-start | bytes 589828
  16.0 15.8 %copy-start.3 = (s32[1,1,128]{2,1,0:T(1,128)S(1)}, s32[1,1,128]{2,1,0:T(1,128)}, u32[]{:S(2)}) copy-start(s32[1,1,128]{2,1,0:T(1,128)} %param.10) | copy-start | bytes 1540
  16.0 15.7 %all-to-all-start = ((bf16[16,4,16,128]{3,2,1,0:T(8,128)(2,1)}), bf16[16,4,16,128]{3,2,1,0:T(8,128)(2,1)S(1)}, u32[]{:S(2)}, u32[]{:S(2)}) async-start(bf16[16,4,16,128]{3,2,1,0:T(8,128)(2,1)} %predict.1), calls=%async_computation | async-start | bytes 524288 | tf_op jit(solution)/shard_map/all_to_all | solution.py:349
